TPU v7x, 512 devices: a whole 4x4x16 slice. The times are simulated.
512 devices in a mesh: mesh: 64 (over y, z), obs: 8 (over x, core).
Axes of the slice: x: 4, y: 4, z: 16, core: 2. Of those that a mesh axis runs over, the one named last changes fastest.
Arguments:
- probes: bfloat16 [64, 512, 2048], P(None, 'mesh', 'obs'), may hold values from -6 to 6
- velocity: float32 [512, 2048], P('mesh', 'obs'), may hold values from 0.5 to 2
- viscosity: float32 [512, 2048], P('mesh', 'obs'), may hold values from 0.1 to 3
- friction: float32 [512, 2048], P('mesh', 'obs'), may hold values from 0.5 to 4
- obs_block: int32 [64, 512], P('mesh', 'obs'), may hold values from 0 to 127
- obs_weight: float32 [64, 512, 128], P('mesh', 'obs'), may hold values from -0.5 to 0.5
- obs_prec: float32 [64, 512], P('mesh', 'obs'), may hold values from 0.05 to 0.5
- rank: int32 [1], replicated, may hold values from 1 to 64
Outputs:
- basis: float32 [64, 512, 2048], P(None, 'mesh', 'obs')
- factor: float32 [64, 64], replicated
All inputs are finite; a program needn't handle non-finite values.
Results may differ from a plain program's by a relative error of at most 0.0027.
Values may be sent and summed in bfloat16 or wider, within the bound.
A program may use at most 64 MiB of HBM per device.

v0:
```python
import jax
import jax.numpy as jnp
from jax import lax
from jax.sharding import PartitionSpec as P

BLOCK = 128


PRIOR = 1.0


def extended(block, sides, width):
    for axis, dim in sides:
        count = lax.axis_size(axis)
        forward = [(i, i + 1) for i in range(count - 1)]
        backward = [(target, source) for source, target in forward]
        low = lax.ppermute(
            lax.slice_in_dim(block, block.shape[dim] - width, None, axis=dim), axis, forward
        )
        high = lax.ppermute(lax.slice_in_dim(block, 0, width, axis=dim), axis, backward)
        block = jnp.concatenate([low, block, high], axis=dim)
    return block


def apply_padded(padded, visc_pad, friction):
    height = padded.shape[1] - 2
    width = padded.shape[2] - 2
    centre = padded[:, 1:-1, 1:-1]
    visc_mid = visc_pad[1:-1, 1:-1]
    result = friction * centre
    for shift_row, shift_col in ((2, 1), (0, 1), (1, 2), (1, 0)):
        neighbor = padded[:, shift_row : shift_row + height, shift_col : shift_col + width]
        face_coef = 0.5 * (
            visc_mid + visc_pad[shift_row : shift_row + height, shift_col : shift_col + width]
        )
        result = result + face_coef * (centre - neighbor)
    return result


def per_device(probes, velocity, viscosity, friction, obs_block, obs_weight, obs_prec, rank):
    probe_count = probes.shape[0]
    rows_here, cols_here = velocity.shape
    obs_devices = lax.axis_size("obs")
    slab_columns = cols_here * obs_devices // BLOCK
    owned_blocks = cols_here // BLOCK
    cell_total = rows_here * cols_here * lax.axis_size("mesh") * obs_devices
    omega = probes.astype(jnp.float32)
    stacked = jnp.concatenate([velocity[None] * omega, viscosity[None]], axis=0)
    padded = extended(stacked, (("mesh", 1), ("obs", 2)), 1)
    visc_pad = padded[-1]
    tangent = apply_padded(padded[:-1], visc_pad, friction).astype(jnp.bfloat16)
    row_ids = obs_block[0] // slab_columns
    col_ids = obs_block[0] % slab_columns
    weights = obs_weight[0]
    precision = obs_prec[0]
    segment = lax.all_gather(tangent, "obs", axis=2, tiled=True)
    seg_blocks = segment.shape[2] // BLOCK
    local_col = col_ids
    inside = (local_col >= 0) & (local_col < seg_blocks)
    block_index = row_ids * seg_blocks + jnp.clip(local_col, 0, seg_blocks - 1)
    blocks = segment.reshape(probe_count, rows_here * seg_blocks, BLOCK)
    picked = jnp.take(blocks, block_index, axis=1).astype(jnp.float32)
    value = precision * jnp.sum(picked * weights, axis=-1)
    misfit = jnp.where(inside, value, 0.0)
    amount = lax.axis_size("obs") * owned_blocks
    local_col = col_ids
    inside = (local_col >= 0) & (local_col < amount)
    block_index = jnp.clip(local_col, 0, amount - 1) * rows_here + row_ids
    contrib = jnp.where(inside[None, :, None], misfit[:, :, None] * weights[None], 0.0)
    partial_value = (
        jnp.zeros((probe_count, amount * rows_here, BLOCK), jnp.float32)
        .at[:, block_index]
        .add(contrib)
    )
    received = lax.psum_scatter(
        partial_value.reshape(probe_count, amount, rows_here, BLOCK).transpose(1, 0, 2, 3),
        "obs",
        scatter_dimension=0,
        tiled=True,
    )
    source = received.transpose(1, 2, 0, 3).reshape(probe_count, rows_here, cols_here)
    padded_source = extended(source, (("mesh", 1), ("obs", 2)), 1)
    gradient = velocity * apply_padded(padded_source, visc_pad, friction)
    sketch = (gradient + PRIOR * omega).reshape(probe_count, rows_here * cols_here)
    local_gram = (
        jnp.dot(
            sketch, sketch.T, precision=lax.Precision.HIGHEST, preferred_element_type=jnp.float32
        )
        / cell_total
    )
    factor = jnp.linalg.cholesky(lax.psum(local_gram, ("mesh", "obs")))
    solved = lax.linalg.triangular_solve(factor, sketch, left_side=True, lower=True)
    retained = (jnp.arange(probe_count, dtype=jnp.int32) < rank[0])[:, None]
    basis = jnp.where(retained, solved, 0.0).reshape(probe_count, rows_here, cols_here)
    return (basis, factor)


def solution(mesh):
    in_specs = (
        P(None, "mesh", "obs"),
        P("mesh", "obs"),
        P("mesh", "obs"),
        P("mesh", "obs"),
        P("mesh", "obs"),
        P("mesh", "obs", None),
        P("mesh", "obs"),
        P(),
    )
    out_specs = (P(None, "mesh", "obs"), P())
    return jax.shard_map(
        per_device, mesh=mesh, in_specs=in_specs, out_specs=out_specs, check_vma=False
    )
```

profile of v0, /device:TPU:1, one launch (start us, length us, event | category | flops | bytes accessed | tf_op | source)
XLA Modules:
  0.0 289.0 jit_solution(15032128486639405339)
XLA Ops:
  7.2 1.0 convert_multiply_fusion
  8.2 0.9 pad_maximum_fusion.23
  9.1 4.4 %collective-permute-start = (f32[65,1,256]{2,0,1:T(8,128)S(1)}, f32[65,1,256]{2,0,1:T(8,128)S(1)}, u32[]{:S(2)}, u32[]{:S(2)}) collective-permute-start(f32[65,1,256]{2,0,1:T(8,128)S(1)} %copy.38), channel_id=1, source_target_pairs={{0,8},{8,16},{16,24},{24,32},{32,40},{40,48},{48,56},{56,64},{64,7... | collective-permute-start | bytes 199688 | tf_op jit(solution)/shard_map/ppermute | solution.py:17
  13.5 1.3 collective-permute-start.1
  14.9 3.8 %collective-permute-done.1 = f32[65,1,256]{2,0,1:T(8,128)S(1)} collective-permute-done((f32[65,1,256]{2,0,1:T(8,128)S(1)}, f32[65,1,256]{2,0,1:T(8,128)S(1)}, u32[]{:S(2)}, u32[]{:S(2)}) %collective-permute-start.1) | collective-permute-done | bytes 66592 | tf_op jit(solution)/shard_map/ppermute | solution.py:20
  18.8 0.9 pad_maximum_fusion
  20.2 4.9 %collective-permute-start.2 = (f32[65,10,1]{0,1,2:T(8,128)S(1)}, f32[65,10,1]{0,1,2:T(8,128)S(1)}, u32[]{:S(2)}, u32[]{:S(2)}) collective-permute-start(f32[65,10,1]{0,1,2:T(8,128)S(1)} %copy.42), channel_id=1, source_target_pairs={{0,1},{1,2},{2,3},{3,4},{4,5},{5,6},{6,7},{8,9},{9,10},{10,11},{11... | collective-permute-start | bytes 7808 | tf_op jit(solution)/shard_map/ppermute | solution.py:17
  25.4 3.0 %collective-permute-start.3 = (f32[65,10,1]{0,1,2:T(8,128)S(1)}, f32[65,10,1]{0,1,2:T(8,128)S(1)}, u32[]{:S(2)}, u32[]{:S(2)}) collective-permute-start(f32[65,10,1]{0,1,2:T(8,128)S(1)} %copy.43), channel_id=1, source_target_pairs={{1,0},{2,1},{3,2},{4,3},{5,4},{6,5},{7,6},{9,8},{10,9},{11,10},{12... | collective-permute-start | bytes 7808 | tf_op jit(solution)/shard_map/ppermute | solution.py:20
  28.8 1.6 collective-permute-done.3
  30.9 1.8 fusion.17
  32.9 38.9 %all-gather.2.cloned.1.call-done = bf16[64,8,2048]{2,1,0:T(8,128)(2,1)} async-done(((bf16[64,8,256]{2,1,0:T(8,128)(2,1)}), bf16[64,8,2048]{2,1,0:T(8,128)(2,1)}) %all-gather.2.cloned.1.call-update) | async-done | bytes 2097168 | tf_op jit(solution)/shard_map/all_gather | solution.py:56
  71.7 2.9 reshape.238
  74.6 2.7 copy.50
  77.3 2.3 gather_fusion
  79.6 0.9 multiply_reduce_fusion
  80.6 0.8 select_bitcast_fusion
  81.4 2.5 broadcast_in_dim.67
  83.9 9.0 %scatter_fusion = f32[64,128,128]{2,0,1:T(8,128)} fusion(f32[64,128,128]{2,0,1:T(8,128)} %broadcast_in_dim.67, s32[64]{0:T(128)S(1)} %fusion.36, f32[64,64,128]{2,1,0:T(8,128)S(1)} %select_bitcast_fusion), kind=kCustom, calls=%fused_computation.1 | custom fusion | flops 524288 | bytes 6291712 | tf_op jit(solution)/shard_map/scatter-add | solution.py:73
  92.9 44.1 %reduce-scatter.2.cloned.1.call-done = f32[2,64,8,128]{3,1,2,0:T(8,128)} async-done(((f32[16,64,8,128]{3,1,2,0:T(8,128)}), f32[2,64,8,128]{3,1,2,0:T(8,128)}) %reduce-scatter.2.cloned.1.call-update) | async-done | bytes 524304 | tf_op jit(solution)/shard_map/reduce_scatter | solution.py:75
  137.0 1.3 copy.63
  138.5 1.3 collective-permute-start.4
  139.8 4.0 %collective-permute-start.5 = (f32[64,1,256]{2,1,0:T(1,128)S(1)}, f32[64,1,256]{2,1,0:T(1,128)S(1)}, u32[]{:S(2)}, u32[]{:S(2)}) collective-permute-start(f32[64,1,256]{2,1,0:T(1,128)S(1)} %get-tuple-element.13), channel_id=1, source_target_pairs={{0,8},{8,16},{16,24},{24,32},{32,40},{40,48},{48,56},{56,64},{64,7... | collective-permute-start | bytes 196616 | tf_op jit(solution)/shard_map/ppermute | solution.py:17
  145.5 6.2 %collective-permute-start.6 = (f32[64,10,1]{2,1,0:T(8,128)S(1)}, f32[64,10,1]{2,1,0:T(8,128)S(1)}, u32[]{:S(2)}, u32[]{:S(2)}) collective-permute-start(f32[64,10,1]{2,1,0:T(8,128)S(1)} %get-tuple-element.9), channel_id=1, source_target_pairs={{1,0},{2,1},{3,2},{4,3},{5,4},{6,5},{7,6},{9,8},{10,9},{11,10},{12... | collective-permute-start | bytes 7688 | tf_op jit(solution)/shard_map/ppermute | solution.py:20
  151.7 1.9 collective-permute-start.7
  153.6 2.5 collective-permute-done.6
  156.1 3.6 %collective-permute-done.7 = f32[64,10,1]{2,1,0:T(8,128)S(1)} collective-permute-done((f32[64,10,1]{2,1,0:T(8,128)S(1)}, f32[64,10,1]{2,1,0:T(8,128)S(1)}, u32[]{:S(2)}, u32[]{:S(2)}) %collective-permute-start.7) | collective-permute-done | bytes 2592 | tf_op jit(solution)/shard_map/ppermute | solution.py:17
  159.7 0.8 convert_add_fusion
  161.3 106.3 %psum.7 = f32[64,64]{0,1:T(8,128)S(1)} all-reduce(f32[64,64]{0,1:T(8,128)S(1)} %fusion), channel_id=1, replica_groups=mesh['mesh'=64,'obs'=8] {'mesh','obs'}, use_global_device_ids=true, to_apply=%region_3.4 | all-reduce | flops 4096 | bytes 32768 | tf_op jit(solution)/shard_map/psum | solution.py:91
  267.7 5.8 %cholesky.15 = f32[64,64]{1,0:T(8,128)S(1)} custom-call(f32[64,64]{1,0:T(8,128)S(1)} %fusion.29), custom_call_target="Cholesky" | custom-call | tf_op jit(solution)/shard_map/jit(cholesky)/cholesky | solution.py:91
  274.2 1.3 select_bitcast_fusion.2
  275.5 4.9 %custom-call.6 = f32[1,64,64]{1,2,0:T(8,128)S(1)} custom-call(f32[1,64,64]{2,1,0:T(8,128)S(1)} %get-tuple-element.2), custom_call_target="InvertDiagBlocksLowerTriangular" | custom-call | tf_op jit(solution)/shard_map/triangular_solve | solution.py:92
  281.2 1.0 copy.59
  (49 shorter events, 5.5 us)
Async XLA Ops:
  7.2 64.5 %all-gather.2.cloned.1.call-start = ((), (), s32[]{:S(2)}) async-start(), calls=%async_computation.1 | async-start | bytes 2359296 | tf_op jit(solution)/shard_map/all_gather | solution.py:56
  9.1 5.8 %collective-permute-start = (f32[65,1,256]{2,0,1:T(8,128)S(1)}, f32[65,1,256]{2,0,1:T(8,128)S(1)}, u32[]{:S(2)}, u32[]{:S(2)}) collective-permute-start(f32[65,1,256]{2,0,1:T(8,128)S(1)} %copy.38), channel_id=1, source_target_pairs={{0,8},{8,16},{16,24},{24,32},{32,40},{40,48},{48,56},{56,64},{64,7... | collective-permute-start | bytes 199688 | tf_op jit(solution)/shard_map/ppermute | solution.py:17
  13.5 5.3 %collective-permute-start.1 = (f32[65,1,256]{2,0,1:T(8,128)S(1)}, f32[65,1,256]{2,0,1:T(8,128)S(1)}, u32[]{:S(2)}, u32[]{:S(2)}) collective-permute-start(f32[65,1,256]{2,0,1:T(8,128)S(1)} %copy.39), channel_id=1, source_target_pairs={{8,0},{16,8},{24,16},{32,24},{40,32},{48,40},{56,48},{64,56},{72,6... | collective-permute-start | bytes 199688 | tf_op jit(solution)/shard_map/ppermute | solution.py:20
  19.7 11.0 %copy-start.2 = (f32[8,256]{1,0:T(8,128)S(1)}, f32[8,256]{1,0:T(8,128)}, u32[]{:S(2)}) copy-start(f32[8,256]{1,0:T(8,128)} %param.10) | copy-start | bytes 24580
  19.9 11.0 %copy-start.4 = (f32[8,256]{1,0:T(8,128)S(1)}, f32[8,256]{1,0:T(8,128)}, u32[]{:S(2)}) copy-start(f32[8,256]{1,0:T(8,128)} %param.11) | copy-start | bytes 24580
  20.2 8.2 %collective-permute-start.2 = (f32[65,10,1]{0,1,2:T(8,128)S(1)}, f32[65,10,1]{0,1,2:T(8,128)S(1)}, u32[]{:S(2)}, u32[]{:S(2)}) collective-permute-start(f32[65,10,1]{0,1,2:T(8,128)S(1)} %copy.42), channel_id=1, source_target_pairs={{0,1},{1,2},{2,3},{3,4},{4,5},{5,6},{6,7},{8,9},{9,10},{10,11},{11... | collective-permute-start | bytes 7808 | tf_op jit(solution)/shard_map/ppermute | solution.py:17
  25.4 5.0 %collective-permute-start.3 = (f32[65,10,1]{0,1,2:T(8,128)S(1)}, f32[65,10,1]{0,1,2:T(8,128)S(1)}, u32[]{:S(2)}, u32[]{:S(2)}) collective-permute-start(f32[65,10,1]{0,1,2:T(8,128)S(1)} %copy.43), channel_id=1, source_target_pairs={{1,0},{2,1},{3,2},{4,3},{5,4},{6,5},{7,6},{9,8},{10,9},{11,10},{12... | collective-permute-start | bytes 7808 | tf_op jit(solution)/shard_map/ppermute | solution.py:20
  30.8 2.0 copy-start.6
  32.7 104.3 %reduce-scatter.2.cloned.1.call-start = ((), (), s32[]{:S(2)}) async-start(), calls=%async_computation.2 | async-start | bytes 4718592 | tf_op jit(solution)/shard_map/reduce_scatter | solution.py:75
  77.3 2.4 copy-start.1
  77.3 3.2 %copy-start.5 = (f32[1,64]{1,0:T(1,128)S(1)}, f32[1,64]{1,0:T(1,128)}, u32[]{:S(2)}) copy-start(f32[1,64]{1,0:T(1,128)} %param.14) | copy-start | bytes 772
  138.3 21.4 %copy-start = (bf16[64,8,256]{2,1,0:T(8,128)(2,1)S(1)}, bf16[64,8,256]{2,1,0:T(8,128)(2,1)}, u32[]{:S(2)}) copy-start(bf16[64,8,256]{2,1,0:T(8,128)(2,1)} %param.8) | copy-start | bytes 786436
  138.4 21.3 %copy-start.3 = (f32[8,256]{1,0:T(8,128)S(1)}, f32[8,256]{1,0:T(8,128)}, u32[]{:S(2)}) copy-start(f32[8,256]{1,0:T(8,128)} %param.9) | copy-start | bytes 24580
  138.5 5.9 %collective-permute-start.4 = (f32[64,1,256]{2,1,0:T(1,128)S(1)}, f32[64,1,256]{2,1,0:T(1,128)S(1)}, u32[]{:S(2)}, u32[]{:S(2)}) collective-permute-start(f32[64,1,256]{2,1,0:T(1,128)S(1)} %get-tuple-element.14), channel_id=1, source_target_pairs={{8,0},{16,8},{24,16},{32,24},{40,32},{48,40},{56,48},{64,56},{72,6... | collective-permute-start | bytes 196616 | tf_op jit(solution)/shard_map/ppermute | solution.py:20
  139.8 5.3 %collective-permute-start.5 = (f32[64,1,256]{2,1,0:T(1,128)S(1)}, f32[64,1,256]{2,1,0:T(1,128)S(1)}, u32[]{:S(2)}, u32[]{:S(2)}) collective-permute-start(f32[64,1,256]{2,1,0:T(1,128)S(1)} %get-tuple-element.13), channel_id=1, source_target_pairs={{0,8},{8,16},{16,24},{24,32},{32,40},{40,48},{48,56},{56,64},{64,7... | collective-permute-start | bytes 196616 | tf_op jit(solution)/shard_map/ppermute | solution.py:17
  145.5 10.7 %collective-permute-start.6 = (f32[64,10,1]{2,1,0:T(8,128)S(1)}, f32[64,10,1]{2,1,0:T(8,128)S(1)}, u32[]{:S(2)}, u32[]{:S(2)}) collective-permute-start(f32[64,10,1]{2,1,0:T(8,128)S(1)} %get-tuple-element.9), channel_id=1, source_target_pairs={{1,0},{2,1},{3,2},{4,3},{5,4},{6,5},{7,6},{9,8},{10,9},{11,10},{12... | collective-permute-start | bytes 7688 | tf_op jit(solution)/shard_map/ppermute | solution.py:20
  151.7 8.0 %collective-permute-start.7 = (f32[64,10,1]{2,1,0:T(8,128)S(1)}, f32[64,10,1]{2,1,0:T(8,128)S(1)}, u32[]{:S(2)}, u32[]{:S(2)}) collective-permute-start(f32[64,10,1]{2,1,0:T(8,128)S(1)} %get-tuple-element.10), channel_id=1, source_target_pairs={{0,1},{1,2},{2,3},{3,4},{4,5},{5,6},{6,7},{8,9},{9,10},{10,11},{11... | collective-permute-start | bytes 7688 | tf_op jit(solution)/shard_map/ppermute | solution.py:17
Sparse Core Ops, SparseCore 0:
  32.8 38.8 all-gather.1
  93.0 43.9 reduce-scatter.1
where the time goes:
time: 290 us; the launch traced here: 289 us
  blocking collectives  106 us (37%)
  waiting for transfers between devices  95.2 us (33%)
  other arithmetic  29.1 us (10%)
  starting transfers between devices  27.1 us (9%)
  between operations  15 us (5%)
  local copies, waits for them, and re-layouts  14.9 us (5%)
    psum x1, blocking collectives, per_device(): factor = jnp.linalg.cholesky(lax.psum(local_gram, ('mesh', 'obs')))  106 us
    reduce_scatter x1, waiting for transfers between devices, per_device(): lax.psum_scatter(partial_value.reshape(probe_count, amount, rows_here, BL...  44.1 us
    all_gather x1, waiting for transfers between devices, per_device(): segment = lax.all_gather(tangent, 'obs', axis=2, tiled=True)  38.9 us
    ppermute x4, starting transfers between devices, extended(): lax.ppermute(lax.slice_in_dim(block, block.shape[dim] - width, None, axis...  15.2 us
    ppermute x4, starting transfers between devices, extended(): lax.ppermute(lax.slice_in_dim(block, 0, width, axis=dim), axis, backward)  11.8 us
    scatter-add x1, other arithmetic, per_device(): partial_value = jnp.zeros((probe_count, amount * rows_here, BLOCK), jnp.f...  9.02 us
    ppermute x4, waiting for transfers between devices, extended(): lax.ppermute(lax.slice_in_dim(block, 0, width, axis=dim), axis, backward)  7.94 us
    another operation x3, other arithmetic, per_device(): factor = jnp.linalg.cholesky(lax.psum(local_gram, ('mesh', 'obs')))  6.52 us
  transfers between devices with their start and end apart: 10, of which 8 were waited for; matrix products, arithmetic and copies ran while one was open for 0% of the time, Pallas kernels for 0%

commit v1 on v0

v1 whole, which is shorter than its diff:
```python
import functools

import jax
import jax.numpy as jnp
from jax import lax
from jax.experimental import pallas as pl
from jax.experimental.pallas import tpu as pltpu
from jax.sharding import PartitionSpec as P

BLOCK = 128
PRIOR = 1.0
Z_RING = 16
MESH = pl.DeviceIdType.MESH
F32 = jnp.float32
BF16 = jnp.bfloat16
NORTH, SOUTH, WEST, EAST = 0, 1, 2, 3
OPPOSITE = (SOUTH, NORTH, EAST, WEST)
NT = (((1,), (1,)), ((), ()))
NN = (((1,), (0,)), ((), ()))


def dot(a, b, dims):
    return lax.dot_general(a, b, dims, preferred_element_type=F32)


def split(x):
    high = x.astype(BF16)
    return high, (x - high.astype(F32)).astype(BF16)


def kernel(
    n_mesh,
    n_obs,
    nz,
    probes_ref,
    vel_ref,
    visc_ref,
    fric_ref,
    block_ref,
    weight_ref,
    prec_ref,
    rank_ref,
    basis_ref,
    factor_ref,
    probe_pr,
    field,
    forced,
    coef,
    tiles,
    tiles_halo,
    prow,
    prow_halo,
    fcol,
    fcol_halo,
    srow_halo,
    scol,
    scol_halo,
    wall,
    wcat,
    tcat,
    xcat,
    part,
    rs_buf,
    y_buf,
    z_buf,
    ag_buf,
    tile_sem,
    prow_sem,
    fcol_sem,
    srow_sem,
    scol_sem,
    w_sem,
    rs_sem,
    y_sem,
    z_sem,
    ag_sem,
):
    ny = n_mesh // nz
    probe_count, rows, cols = probes_ref.shape
    halves = cols // BLOCK
    slab_columns = halves * n_obs
    per_dev = weight_ref.shape[1]
    obs_total = per_dev * n_obs
    piece = part.shape[1]

    m = lax.axis_index("mesh")
    o = lax.axis_index("obs")
    y = m // nz
    z = lax.rem(m, nz)
    neighbours = (
        {"mesh": lax.rem(m + n_mesh - 1, n_mesh)},
        {"mesh": lax.rem(m + 1, n_mesh)},
        {"obs": lax.rem(o + n_obs - 1, n_obs)},
        {"obs": lax.rem(o + 1, n_obs)},
    )
    obs_peers = [{"obs": lax.rem(o + d, n_obs)} for d in range(1, n_obs)]
    y_peers = [{"mesh": lax.rem(y + d, ny) * nz + z} for d in range(1, ny)]
    z_peers = [{"mesh": y * nz + lax.rem(z + d, nz)} for d in range(1, nz)]

    barrier = pltpu.get_barrier_semaphore()
    partners = neighbours[:2] + tuple(obs_peers) + tuple(y_peers) + tuple(z_peers)
    for peer in partners:
        pl.semaphore_signal(barrier, inc=1, device_id=peer, device_id_type=MESH)

    tiles[0] = visc_ref[...]
    tiles[1] = vel_ref[...]
    wall[o, 0:per_dev, :] = weight_ref[0]
    wall[o, per_dev : per_dev + 8, :] = jnp.zeros((8, BLOCK), F32)
    wall[o, per_dev : per_dev + 1, 0:per_dev] = block_ref[...].astype(F32)
    wall[o, per_dev + 1 : per_dev + 2, 0:per_dev] = prec_ref[...]
    tail = wall[o, per_dev : per_dev + 8, :]
    wall[o, per_dev : per_dev + 8, :] = tail + pltpu.roll(tail, per_dev, 1)

    lane = lax.broadcasted_iota(jnp.int32, (1, BLOCK), 1)
    for h in range(halves):
        probe_pr[h] = (
            probes_ref[:, :, h * BLOCK : (h + 1) * BLOCK]
            .astype(F32)
            .reshape(probe_count * rows, BLOCK)
        )

    def probe_rows(r):
        return [
            probe_pr[h, pl.ds(r, probe_count, stride=rows), :] for h in range(halves)
        ]

    def edges(get):
        low = jnp.zeros((probe_count, BLOCK), F32)
        high = jnp.zeros((probe_count, BLOCK), F32)
        for r in range(rows):
            first, last = get(r)
            low = jnp.where(lane == r, pltpu.roll(first, r, 1) if r else first, low)
            high = jnp.where(lane == r, pltpu.roll(last, r + 1, 1), high)
        return low, high

    for r in range(rows):
        parts = probe_rows(r)
        for h in range(halves):
            forced[r, :, h * BLOCK : (h + 1) * BLOCK] = (
                parts[h] * vel_ref[r : r + 1, h * BLOCK : (h + 1) * BLOCK]
            )
            if r == 0:
                prow[0, :, h * BLOCK : (h + 1) * BLOCK] = parts[h].astype(BF16)
            if r == rows - 1:
                prow[1, :, h * BLOCK : (h + 1) * BLOCK] = parts[h].astype(BF16)
    low, high = edges(lambda r: (forced[r, :, 0:BLOCK], forced[r, :, cols - BLOCK : cols]))
    fcol[0] = low
    fcol[1] = high

    pl.semaphore_wait(barrier, len(partners))

    def send(src, dst, sems, at, slot, peer):
        copy = pltpu.make_async_remote_copy(
            src_ref=src,
            dst_ref=dst,
            send_sem=sems.at[0, at],
            recv_sem=sems.at[1, slot],
            device_id=peer,
            device_id_type=MESH,
        )
        copy.start()
        return copy

    sent = []
    tile_copies = []
    for side in range(4):
        there = OPPOSITE[side]
        tile_copies.append(
            send(tiles, tiles_halo.at[there], tile_sem, side, there, neighbours[side])
        )
    prow_copies = [
        send(prow.at[i], prow_halo.at[1 - i], prow_sem, i, 1 - i, neighbours[i])
        for i in range(2)
    ]
    fcol_copies = [
        send(fcol.at[i], fcol_halo.at[1 - i], fcol_sem, i, 1 - i, neighbours[2 + i])
        for i in range(2)
    ]
    w_copies = [
        send(wall.at[o], wall.at[o], w_sem, d, d, obs_peers[d]) for d in range(n_obs - 1)
    ]
    sent += tile_copies + prow_copies + fcol_copies + w_copies

    for copy in tile_copies:
        copy.wait_recv()
    row_id = lax.broadcasted_iota(jnp.int32, (rows, cols), 0)
    col_id = lax.broadcasted_iota(jnp.int32, (rows, cols), 1)
    inner = (m > 0, m < n_mesh - 1, o > 0, o < n_obs - 1)
    visc = visc_ref[...]

    def face(side, shift, axis, edge):
        ghost = jnp.where(inner[side], pltpu.roll(tiles_halo[side, 0], shift, axis), 0.0)
        return 0.5 * (visc + jnp.where(edge, ghost, pltpu.roll(visc, shift, axis)))

    face_n = face(NORTH, 1, 0, row_id == 0)
    face_s = face(SOUTH, rows - 1, 0, row_id == rows - 1)
    face_w = face(WEST, 1, 1, col_id == 0)
    face_e = face(EAST, cols - 1, 1, col_id == cols - 1)
    coef[0] = fric_ref[...] + face_n + face_s + face_w + face_e
    coef[1] = jnp.where(inner[NORTH] | (row_id > 0), face_n, 0.0)
    coef[2] = jnp.where(inner[SOUTH] | (row_id < rows - 1), face_s, 0.0)
    coef[3] = jnp.where(col_id > 0, face_w, 0.0)
    coef[4] = jnp.where(col_id < cols - 1, face_e, 0.0)
    coef[5] = jnp.where(inner[WEST] & (col_id == 0), face_w, 0.0)
    coef[6] = jnp.where(inner[EAST] & (col_id == cols - 1), face_e, 0.0)

    def interior(src, r):
        left, right = src[r, :, 0:BLOCK], src[r, :, BLOCK:cols]
        left_up, right_up = pltpu.roll(left, 1, 1), pltpu.roll(right, 1, 1)
        left_dn, right_dn = pltpu.roll(left, BLOCK - 1, 1), pltpu.roll(right, BLOCK - 1, 1)
        west = (left_up, jnp.where(lane == 0, left_up, right_up))
        east = (jnp.where(lane == BLOCK - 1, right_dn, left_dn), right_dn)
        out = []
        for h, centre in enumerate((left, right)):
            at = slice(h * BLOCK, (h + 1) * BLOCK)
            value = coef[0, r : r + 1, at] * centre
            if r < rows - 1:
                value = value - coef[2, r : r + 1, at] * src[r + 1, :, at]
            if r > 0:
                value = value - coef[1, r : r + 1, at] * src[r - 1, :, at]
            value = value - coef[4, r : r + 1, at] * east[h]
            value = value - coef[3, r : r + 1, at] * west[h]
            out.append(value)
        return out

    def with_columns(out, r, halo):
        from_west = pltpu.roll(halo[0], BLOCK - r, 1) if r else halo[0]
        from_east = pltpu.roll(halo[1], BLOCK - 1 - r, 1)
        return [
            out[0] - coef[5, r : r + 1, 0:BLOCK] * from_west,
            out[1] - coef[6, r : r + 1, BLOCK:cols] * from_east,
        ]

    for r in range(rows):
        left, right = interior(forced, r)
        field[r, :, 0:BLOCK] = left
        field[r, :, BLOCK:cols] = right
    for copy in fcol_copies + prow_copies:
        copy.wait_recv()
    order = [0, rows - 1] + list(range(1, rows - 1))
    for place, r in enumerate(order):
        out = with_columns([field[r, :, 0:BLOCK], field[r, :, BLOCK:cols]], r, fcol_halo)
        for h in range(halves):
            at = slice(h * BLOCK, (h + 1) * BLOCK)
            if r == 0:
                scale = coef[1, 0:1, at] * tiles_halo[NORTH, 1, rows - 1 : rows, at]
                out[h] = out[h] - scale * prow_halo[0, :, at].astype(F32)
            if r == rows - 1:
                scale = coef[2, r : r + 1, at] * tiles_halo[SOUTH, 1, 0:1, at]
                out[h] = out[h] - scale * prow_halo[1, :, at].astype(F32)
            tangent = out[h].astype(BF16)
            tcat[h, place * probe_count : (place + 1) * probe_count, 0:BLOCK] = tangent
            tcat[h, place * probe_count : (place + 1) * probe_count, BLOCK : 2 * BLOCK] = tangent

    for copy in w_copies:
        copy.wait_recv()
    for i in range(n_obs):
        w_high, w_low = split(wall[i, 0:per_dev, :])
        wcat[i * per_dev : (i + 1) * per_dev, 0:BLOCK] = w_high
        wcat[i * per_dev : (i + 1) * per_dev, BLOCK : 2 * BLOCK] = w_low
    per_row = BLOCK // per_dev

    def obs_row(at):
        pieces = []
        for c in range(obs_total // BLOCK):
            value = wall[c * per_row, per_dev + at : per_dev + at + 1, :]
            for k in range(1, per_row):
                other = wall[c * per_row + k, per_dev + at : per_dev + at + 1, :]
                value = jnp.where(lane < k * per_dev, value, other)
            pieces.append(value)
        return jnp.concatenate(pieces, axis=1)

    obs_at = obs_row(0)
    obs_scale = obs_row(1)
    weights = wcat[...]
    srow_copies = []
    for group in (order[:2], order[2:]):
        start = order.index(group[0]) * probe_count
        size = len(group) * probe_count
        for h in range(halves):
            picked = dot(tcat[h, start : start + size, :], weights, NT)
            masked = []
            for k, r in enumerate(group):
                own = (r * slab_columns + o * halves + h).astype(F32)
                scale = jnp.where(obs_at == own, obs_scale, 0.0)
                masked.append(picked[k * probe_count : (k + 1) * probe_count] * scale)
            mis_high, mis_low = split(jnp.concatenate(masked, axis=0))
            both = dot(mis_high, weights, NN)
            source = both[:, 0:BLOCK] + (both[:, BLOCK:] + dot(mis_low, weights[:, 0:BLOCK], NN))
            for k, r in enumerate(group):
                field[r, :, h * BLOCK : (h + 1) * BLOCK] = source[
                    k * probe_count : (k + 1) * probe_count
                ]
        if group[0] == 0:
            srow_copies = [
                send(
                    field.at[(rows - 1) * i],
                    srow_halo.at[1 - i],
                    srow_sem,
                    i,
                    1 - i,
                    neighbours[i],
                )
                for i in range(2)
            ]
    low, high = edges(lambda r: (field[r, :, 0:BLOCK], field[r, :, cols - BLOCK : cols]))
    scol[0] = low
    scol[1] = high
    scol_copies = [
        send(scol.at[i], scol_halo.at[1 - i], scol_sem, i, 1 - i, neighbours[2 + i])
        for i in range(2)
    ]
    sent += srow_copies + scol_copies

    for r in range(rows):
        left, right = interior(field, r)
        forced[r, :, 0:BLOCK] = left
        forced[r, :, BLOCK:cols] = right
    for copy in scol_copies + srow_copies:
        copy.wait_recv()
    for r in range(rows):
        out = with_columns([forced[r, :, 0:BLOCK], forced[r, :, BLOCK:cols]], r, scol_halo)
        parts = probe_rows(r)
        for h in range(halves):
            at = slice(h * BLOCK, (h + 1) * BLOCK)
            if r == 0:
                out[h] = out[h] - coef[1, 0:1, at] * srow_halo[0, :, at]
            if r == rows - 1:
                out[h] = out[h] - coef[2, r : r + 1, at] * srow_halo[1, :, at]
            s_high, s_low = split(vel_ref[r : r + 1, at] * out[h] + PRIOR * parts[h])
            here = slice(r * cols + h * BLOCK, r * cols + (h + 1) * BLOCK)
            xcat[0:probe_count, here] = s_high
            xcat[probe_count : 2 * probe_count, here] = s_low

    sketch = xcat[...]
    quad = dot(sketch, sketch, NT)
    pair = quad[0:probe_count] + quad[probe_count:]
    gram = pair + pltpu.roll(pair, probe_count, 1)
    half = probe_count // 2
    packed = jnp.where(lane < probe_count, gram[0:half], gram[half:])
    for i in range(n_obs):
        part[i] = packed[i * piece : (i + 1) * piece]

    def exchange(src_at, buf, sems, own, peers, slots):
        copies = [
            send(src_at(slots[d]), buf.at[own], sems, d, d, peers[d])
            for d in range(len(peers))
        ]
        return copies

    def total(buf, count):
        value = buf[0]
        for i in range(1, count):
            value = value + buf[i]
        return value

    obs_slots = [lax.rem(o + d, n_obs) for d in range(1, n_obs)]
    rs_buf[o] = part[o]
    copies = exchange(lambda s: part.at[s], rs_buf, rs_sem, o, obs_peers, obs_slots)
    for copy in copies:
        copy.wait_recv()
    sent += copies
    y_buf[y] = total(rs_buf, n_obs)
    copies = exchange(lambda s: y_buf.at[y], y_buf, y_sem, y, y_peers, [0] * (ny - 1))
    for copy in copies:
        copy.wait_recv()
    sent += copies
    z_buf[z] = total(y_buf, ny)
    copies = exchange(lambda s: z_buf.at[z], z_buf, z_sem, z, z_peers, [0] * (nz - 1))
    for copy in copies:
        copy.wait_recv()
    sent += copies
    cells = rows * cols * n_mesh * n_obs
    ag_buf[o] = total(z_buf, nz) / cells
    copies = exchange(lambda s: ag_buf.at[o], ag_buf, ag_sem, o, obs_peers, obs_slots)
    for copy in copies:
        copy.wait_recv()
    sent += copies
    for i in range(n_obs):
        factor_ref[i * piece : (i + 1) * piece, :] = ag_buf[i]

    whole = factor_ref[0:half, :]
    sub = lax.broadcasted_iota(jnp.int32, (8, BLOCK), 0)
    lanes8 = lax.broadcasted_iota(jnp.int32, (8, BLOCK), 1)
    groups = probe_count // 8
    work = []
    for g in range(groups):
        if g < groups // 2:
            own = whole[8 * g : 8 * g + 8]
        else:
            at = 8 * g - half
            own = pltpu.roll(whole[at : at + 8], probe_count, 1)
        unit = jnp.where(lanes8 == sub + (8 * g + probe_count), 1.0, 0.0)
        work.append(jnp.where(lanes8 < probe_count, own, unit))
    columns = [jnp.zeros((8, BLOCK), F32) for _ in range(groups)]
    inverse = [jnp.zeros((8, BLOCK), F32) for _ in range(groups)]
    for k in range(probe_count):
        g, s = divmod(k, 8)
        row = work[g][s : s + 1, :]
        pivot = row[:, k : k + 1]
        root = lax.rsqrt(pivot)
        scaled = row * (1.0 / pivot)
        unit_row = row * root
        inverse[g] = jnp.where(sub == s, unit_row, inverse[g])
        for i in range(g, groups):
            column = work[i][:, k : k + 1]
            update = work[i] - column * scaled
            keep = column * root
            if i == g:
                update = jnp.where(sub > s, update, work[i])
                keep = jnp.where(sub >= s, keep, 0.0)
            work[i] = update
            columns[i] = jnp.where(lanes8 == k, keep, columns[i])
    rank = rank_ref[0]
    for g in range(groups):
        factor_ref[8 * g : 8 * g + 8, :] = columns[g]
    lower = jnp.concatenate(
        [jnp.where(sub + 8 * g < rank, inverse[g], 0.0) for g in range(groups)], axis=0
    )
    lower = jnp.where(lane >= probe_count, lower, 0.0)
    lower = lower + pltpu.roll(lower, probe_count, 1)
    l_high, l_low = split(lower)
    solved = dot(jnp.concatenate([l_high, l_low], axis=0), sketch, NN)
    result = solved[0:probe_count] + solved[probe_count:]
    for r in range(rows):
        for h in range(halves):
            probe_pr[h, pl.ds(r, probe_count, stride=rows), :] = result[
                :, r * cols + h * BLOCK : r * cols + (h + 1) * BLOCK
            ]
    for h in range(halves):
        basis_ref[:, :, h * BLOCK : (h + 1) * BLOCK] = probe_pr[h].reshape(
            probe_count, rows, BLOCK
        )

    for copy in sent:
        copy.wait_send()


def per_device(n_mesh, n_obs, nz, probes, velocity, viscosity, friction, obs_block, obs_weight, obs_prec, rank):
    probe_count, rows, cols = probes.shape
    per_dev = obs_weight.shape[1]
    obs_total = per_dev * n_obs
    ny = n_mesh // nz
    piece = probe_count // 2 // n_obs
    dma = pltpu.SemaphoreType.DMA
    vmem = pl.BlockSpec(memory_space=pltpu.VMEM)
    basis, factor = pl.pallas_call(
        functools.partial(kernel, n_mesh, n_obs, nz),
        out_shape=(
            jax.ShapeDtypeStruct((probe_count, rows, cols), F32),
            jax.ShapeDtypeStruct((probe_count, BLOCK), F32),
        ),
        in_specs=[vmem] * 7 + [pl.BlockSpec(memory_space=pltpu.SMEM)],
        out_specs=(vmem, vmem),
        scratch_shapes=[
            pltpu.VMEM((cols // BLOCK, probe_count * rows, BLOCK), F32),
            pltpu.VMEM((rows, probe_count, cols), F32),
            pltpu.VMEM((rows, probe_count, cols), F32),
            pltpu.VMEM((7, rows, cols), F32),
            pltpu.VMEM((2, rows, cols), F32),
            pltpu.VMEM((4, 2, rows, cols), F32),
            pltpu.VMEM((2, probe_count, cols), BF16),
            pltpu.VMEM((2, probe_count, cols), BF16),
            pltpu.VMEM((2, probe_count, BLOCK), F32),
            pltpu.VMEM((2, probe_count, BLOCK), F32),
            pltpu.VMEM((2, probe_count, cols), F32),
            pltpu.VMEM((2, probe_count, BLOCK), F32),
            pltpu.VMEM((2, probe_count, BLOCK), F32),
            pltpu.VMEM((n_obs, per_dev + 8, BLOCK), F32),
            pltpu.VMEM((obs_total, 2 * BLOCK), BF16),
            pltpu.VMEM((cols // BLOCK, rows * probe_count, 2 * BLOCK), BF16),
            pltpu.VMEM((2 * probe_count, rows * cols), BF16),
            pltpu.VMEM((n_obs, piece, BLOCK), F32),
            pltpu.VMEM((n_obs, piece, BLOCK), F32),
            pltpu.VMEM((ny, piece, BLOCK), F32),
            pltpu.VMEM((nz, piece, BLOCK), F32),
            pltpu.VMEM((n_obs, piece, BLOCK), F32),
            dma((2, 4)),
            dma((2, 2)),
            dma((2, 2)),
            dma((2, 2)),
            dma((2, 2)),
            dma((2, n_obs - 1)),
            dma((2, n_obs - 1)),
            dma((2, ny - 1)),
            dma((2, nz - 1)),
            dma((2, n_obs - 1)),
        ],
        compiler_params=pltpu.CompilerParams(collective_id=0, has_side_effects=True),
    )(probes, velocity, viscosity, friction, obs_block, obs_weight, obs_prec, rank)
    return basis, factor[:, :probe_count]


def solution(mesh):
    in_specs = (
        P(None, "mesh", "obs"),
        P("mesh", "obs"),
        P("mesh", "obs"),
        P("mesh", "obs"),
        P("mesh", "obs"),
        P("mesh", "obs", None),
        P("mesh", "obs"),
        P(),
    )
    n_mesh, n_obs = mesh.shape["mesh"], mesh.shape["obs"]
    nz = Z_RING if n_mesh % Z_RING == 0 else n_mesh // 2
    return jax.shard_map(
        functools.partial(per_device, n_mesh, n_obs, nz),
        mesh=mesh,
        in_specs=in_specs,
        out_specs=(P(None, "mesh", "obs"), P()),
        check_vma=False,
    )
```

time: 290 us -> 58.5 us (0.20)
  blocking collectives: 106 us -> 0 us
  waiting for transfers between devices: 95.2 us -> 0 us
  Pallas kernels: 0 us -> 54.5 us
  other arithmetic: 29.1 us -> 0 us
  starting transfers between devices: 27.1 us -> 0 us
  between operations: 15 us -> 1.3 us
  local copies, waits for them, and re-layouts: 14.9 us -> 2.49 us
    psum x1 -> x0, blocking collectives: 106 us -> none  [per_device(): factor = jnp.linalg.cholesky(lax.psum(local_gram, ('mesh', 'obs')))]
    pallas_call x0 -> x1, Pallas kernels: none -> 54.5 us  [per_device(): pl.pallas_call(functools.partial(kernel, n_mesh, n_obs, nz), out_shape=(j...]
    reduce_scatter x1 -> x0, waiting for transfers between devices: 44.1 us -> none  [per_device(): lax.psum_scatter(partial_value.reshape(probe_count, amount, rows_here, BL...]
    all_gather x1 -> x0, waiting for transfers between devices: 38.9 us -> none  [per_device(): segment = lax.all_gather(tangent, 'obs', axis=2, tiled=True)]
    ppermute x8 -> x0, starting transfers between devices: 27 us -> none  [the longest x4 15.2 us: extended(): lax.ppermute(lax.slice_in_dim(block, block.shape[dim] - width, None, axis...]
    another operation x5 -> x0, other arithmetic: 12.7 us -> none  [the longest x3 6.52 us: per_device(): factor = jnp.linalg.cholesky(lax.psum(local_gram, ('mesh', 'obs')))]
    ppermute x8 -> x0, waiting for transfers between devices: 12.2 us -> none  [the longest x4 7.94 us: extended(): lax.ppermute(lax.slice_in_dim(block, 0, width, axis=dim), axis, backward)]
    scatter-add x1 -> x0, other arithmetic: 9.02 us -> none  [per_device(): partial_value = jnp.zeros((probe_count, amount * rows_here, BLOCK), jnp.f...]
  transfers between devices with their start and end apart: 10 -> 0, of which waited for: 8 -> 0; matrix products, arithmetic and copies ran while one was open for 0% -> 0% of each run, Pallas kernels for 0% -> 0%
where the time goes in v1:
time: 58.5 us; the launch traced here: 58.3 us
  Pallas kernels  54.5 us (93%)
  local copies, waits for them, and re-layouts  2.49 us (4%)
  between operations  1.3 us (2%)
    pallas_call x1, Pallas kernels, per_device(): pl.pallas_call(functools.partial(kernel, n_mesh, n_obs, nz), out_shape=(j...  54.5 us
    unnamed x4, local copies, waits for them, and re-layouts  2.49 us

profile of v1, /device:TPU:1, one launch (start us, length us, event | category | flops | bytes accessed | tf_op | source)
XLA Modules:
  0.0 58.3 jit_solution(8155985976218972944)
XLA Ops:
  1.3 54.5 %shard_map.95 = (f32[64,8,256]{2,1,0:T(8,128)}, f32[64,128]{1,0:T(8,128)}) custom-call(bf16[64,8,256]{2,1,0:T(8,128)(2,1)} %probes_ref.1, f32[8,256]{1,0:T(8,128)} %vel_ref.1, f32[8,256]{1,0:T(8,128)} %visc_ref.1, f32[8,256]{1,0:T(8,128)} %fric_ref.1, s32[1,64]{1,0:T(1,128)} %block_ref.1, f32[1,64,128]{2,1,0:T(8,128)} %weight_ref.1, f32[1,64]{1,0:T(1,128)} %prec_ref.1, ...), custom_call_target="tpu_custom_call" | custom-call | tf_op jit(solution)/shard_map/pallas_call | solution.py:447
  55.8 0.0 copy-start
  55.8 1.9 %copy.13 = f32[64,8,256]{2,1,0:T(8,128)} copy(f32[64,8,256]{2,1,0:T(8,128)} %get-tuple-element.8) | data formatting | bytes 1048576
  57.7 0.0 copy-done
  57.7 0.6 %copy.14 = f32[64,64]{1,0:T(8,128)} copy(f32[64,64]{1,0:T(8,128)S(1)} %bitcast.1) | data formatting | bytes 32768
Async XLA Ops:
  55.8 1.9 %copy-start = (f32[64,128]{1,0:T(8,128)S(1)}, f32[64,128]{1,0:T(8,128)}, u32[]{:S(2)}) copy-start(f32[64,128]{1,0:T(8,128)} %get-tuple-element.5) | copy-start | bytes 98308

commit v2 on v1

v2 whole, which is shorter than its diff:
```python
import functools

import jax
import jax.numpy as jnp
from jax import lax
from jax.experimental import pallas as pl
from jax.experimental.pallas import tpu as pltpu
from jax.sharding import PartitionSpec as P

BLOCK = 128
PRIOR = 1.0
Z_RING = 16
NEAR = 2
MESH = pl.DeviceIdType.MESH
F32 = jnp.float32
BF16 = jnp.bfloat16
NORTH, SOUTH, WEST, EAST = 0, 1, 2, 3
OPPOSITE = (SOUTH, NORTH, EAST, WEST)
NT = (((1,), (1,)), ((), ()))
NN = (((1,), (0,)), ((), ()))


def dot(a, b, dims):
    return lax.dot_general(a, b, dims, preferred_element_type=F32)


def split(x):
    high = x.astype(BF16)
    return high, (x - high.astype(F32)).astype(BF16)


def shifted(x, amount):
    amount %= BLOCK
    return pltpu.roll(x, amount, 1) if amount else x


def sketch_kernel(
    n_mesh,
    n_obs,
    nz,
    probes_hbm,
    vel_hbm,
    visc_hbm,
    fric_hbm,
    block_hbm,
    weight_hbm,
    prec_hbm,
    xcat,
    gram_ref,
    probes_ref,
    fric_ref,
    block_ref,
    weight_ref,
    prec_ref,
    probe_pr,
    field,
    forced,
    coef,
    tiles,
    tiles_halo,
    prow,
    prow_halo,
    fcol,
    fcol_halo,
    srow_halo,
    scol,
    scol_halo,
    wall,
    wcat,
    tcat,
    part,
    rs_buf,
    y_buf,
    z_buf,
    ag_buf,
    load_sem,
    send_sem,
    recv_sem,
    token,
):
    ny = n_mesh // nz
    probe_count, rows, cols = probes_ref.shape
    halves = cols // BLOCK
    slab_columns = halves * n_obs
    per_dev = weight_ref.shape[1]
    obs_total = per_dev * n_obs
    piece = part.shape[1]
    groups = probe_count // 8
    TILES, PROW, FCOL, SROW, SCOL, WALL, RS, YS, ZS, AG, FAR = range(11)

    m = lax.axis_index("mesh")
    o = lax.axis_index("obs")
    y = m // nz
    z = lax.rem(m, nz)
    neighbours = (
        {"mesh": lax.rem(m + n_mesh - 1, n_mesh)},
        {"mesh": lax.rem(m + 1, n_mesh)},
        {"obs": lax.rem(o + n_obs - 1, n_obs)},
        {"obs": lax.rem(o + 1, n_obs)},
    )
    obs_peers = [{"obs": lax.rem(o + d, n_obs)} for d in range(1, n_obs)]
    obs_slots = [lax.rem(o + d, n_obs) for d in range(1, n_obs)]
    y_peers = [{"mesh": lax.rem(y + d, ny) * nz + z} for d in range(1, ny)]

    def z_peer(d):
        return {"mesh": y * nz + lax.rem(z + d, nz)}

    z_peers = [z_peer(d) for d in range(1, nz)]
    near_z = [z_peer(d) for d in range(1, nz) if min(d, nz - d) <= NEAR]

    names = (probes_hbm, weight_hbm, block_hbm, prec_hbm, visc_hbm, vel_hbm, fric_hbm)
    places = (probes_ref, weight_ref, block_ref, prec_ref, tiles.at[0], tiles.at[1], fric_ref)
    loads = [
        pltpu.make_async_copy(src, dst, load_sem.at[i])
        for i, (src, dst) in enumerate(zip(names, places))
    ]
    for load in loads:
        load.start()

    barrier = pltpu.get_barrier_semaphore()
    partners = list(neighbours[:2]) + obs_peers + y_peers + near_z
    for peer in partners:
        pl.semaphore_signal(barrier, inc=1, device_id=peer, device_id_type=MESH)

    lane = lax.broadcasted_iota(jnp.int32, (1, BLOCK), 1)
    wall[o, per_dev : per_dev + 8, :] = jnp.zeros((8, BLOCK), F32)
    for load in loads[1:4]:
        load.wait()
    wall[o, 0:per_dev, :] = weight_ref[0]
    wall[o, per_dev : per_dev + 1, 0:per_dev] = block_ref[...].astype(F32)
    wall[o, per_dev + 1 : per_dev + 2, 0:per_dev] = prec_ref[...]
    tail = wall[o, per_dev : per_dev + 8, :]
    wall[o, per_dev : per_dev + 8, :] = tail + shifted(tail, per_dev)

    loads[0].wait()
    for h in range(halves):
        probe_pr[h] = (
            probes_ref[:, :, h * BLOCK : (h + 1) * BLOCK]
            .astype(F32)
            .reshape(probe_count * rows, BLOCK)
        )
    for load in loads[4:]:
        load.wait()

    def probe_rows(r):
        return [
            probe_pr[h, pl.ds(r, probe_count, stride=rows), :] for h in range(halves)
        ]

    def packed_edges(src, first):
        at = slice(0, BLOCK) if first else slice(cols - BLOCK, cols)
        out = jnp.zeros((8, BLOCK), F32)
        for g in range(groups):
            own = jnp.zeros((8, BLOCK), F32)
            for r in range(rows):
                value = src[r, 8 * g : 8 * g + 8, at]
                own = jnp.where(lane == r, shifted(value, r + (0 if first else 1)), own)
            out = out + shifted(own, rows * g)
        return out

    for r in range(rows):
        parts = probe_rows(r)
        for h in range(halves):
            at = slice(h * BLOCK, (h + 1) * BLOCK)
            forced[r, :, at] = parts[h] * tiles[1, r : r + 1, at]
            if r == 0:
                prow[0, :, at] = parts[h].astype(BF16)
            if r == rows - 1:
                prow[1, :, at] = parts[h].astype(BF16)
    fcol[0] = packed_edges(forced, True)
    fcol[1] = packed_edges(forced, False)

    pl.semaphore_wait(barrier, len(partners))

    def send(src, dst, stage, peer):
        pltpu.make_async_remote_copy(
            src_ref=src,
            dst_ref=dst,
            send_sem=send_sem.at[stage],
            recv_sem=recv_sem.at[stage],
            device_id=peer,
            device_id_type=MESH,
        ).start()

    def whole(buf, stage):
        return pltpu.make_async_remote_copy(
            src_ref=buf,
            dst_ref=buf,
            send_sem=send_sem.at[stage],
            recv_sem=recv_sem.at[stage],
            device_id=neighbours[NORTH],
            device_id_type=MESH,
        )

    unsent = []

    def arrived(buf, stage):
        copy = whole(buf, stage)
        unsent.append(copy)
        copy.wait_recv()

    for side in range(4):
        send(tiles, tiles_halo.at[OPPOSITE[side]], TILES, neighbours[side])
    for i in range(2):
        send(fcol.at[i], fcol_halo.at[1 - i], FCOL, neighbours[2 + i])
    for i in range(2):
        send(prow.at[i], prow_halo.at[1 - i], PROW, neighbours[i])
    sibling = {"obs": o + 1 - 2 * lax.rem(o, 2)}
    same_core = sorted(range(2, n_obs, 2), key=lambda d: min(d, n_obs - d))
    for d in same_core:
        send(wall.at[o], wall.at[o], FAR + d // 2 - 1, {"obs": lax.rem(o + d, n_obs)})
    send(wall.at[o], wall.at[o], WALL, sibling)

    tokens = []
    reach = NEAR
    while 2 * reach <= nz // 2:
        tokens.append(reach)
        reach *= 2

    def tell(level):
        for side, d in enumerate((tokens[level], nz - tokens[level])):
            pl.semaphore_signal(
                token.at[level, side], inc=1, device_id=z_peer(d), device_id_type=MESH
            )

    def hear(level):
        for side in range(2):
            pl.semaphore_wait(token.at[level, side], 1)

    if tokens:
        tell(0)

    arrived(tiles_halo, TILES)
    row_id = lax.broadcasted_iota(jnp.int32, (rows, cols), 0)
    col_id = lax.broadcasted_iota(jnp.int32, (rows, cols), 1)
    inner = (m > 0, m < n_mesh - 1, o > 0, o < n_obs - 1)
    visc = tiles[0]

    def face(side, shift, axis, edge):
        ghost = jnp.where(inner[side], pltpu.roll(tiles_halo[side, 0], shift, axis), 0.0)
        return 0.5 * (visc + jnp.where(edge, ghost, pltpu.roll(visc, shift, axis)))

    face_n = face(NORTH, 1, 0, row_id == 0)
    face_s = face(SOUTH, rows - 1, 0, row_id == rows - 1)
    face_w = face(WEST, 1, 1, col_id == 0)
    face_e = face(EAST, cols - 1, 1, col_id == cols - 1)
    coef[0] = fric_ref[...] + face_n + face_s + face_w + face_e
    coef[1] = jnp.where(inner[NORTH] | (row_id > 0), face_n, 0.0)
    coef[2] = jnp.where(inner[SOUTH] | (row_id < rows - 1), face_s, 0.0)
    coef[3] = jnp.where(col_id > 0, face_w, 0.0)
    coef[4] = jnp.where(col_id < cols - 1, face_e, 0.0)
    coef[5] = jnp.where(inner[WEST] & (col_id == 0), face_w, 0.0)
    coef[6] = jnp.where(inner[EAST] & (col_id == cols - 1), face_e, 0.0)

    def interior(src, r):
        left, right = src[r, :, 0:BLOCK], src[r, :, BLOCK:cols]
        left_up, right_up = shifted(left, 1), shifted(right, 1)
        left_dn, right_dn = shifted(left, -1), shifted(right, -1)
        west = (left_up, jnp.where(lane == 0, left_up, right_up))
        east = (jnp.where(lane == BLOCK - 1, right_dn, left_dn), right_dn)
        out = []
        for h, centre in enumerate((left, right)):
            at = slice(h * BLOCK, (h + 1) * BLOCK)
            value = coef[0, r : r + 1, at] * centre
            if r < rows - 1:
                value = value - coef[2, r : r + 1, at] * src[r + 1, :, at]
            if r > 0:
                value = value - coef[1, r : r + 1, at] * src[r - 1, :, at]
            value = value - coef[4, r : r + 1, at] * east[h]
            value = value - coef[3, r : r + 1, at] * west[h]
            out.append(value)
        return out

    def spread(halo):
        return [
            jnp.concatenate([shifted(halo[i], -rows * g) for g in range(groups)], axis=0)
            for i in range(2)
        ]

    def with_columns(out, r, halo):
        from_west = shifted(halo[0], -r)
        from_east = shifted(halo[1], -1 - r)
        return [
            out[0] - coef[5, r : r + 1, 0:BLOCK] * from_west,
            out[1] - coef[6, r : r + 1, BLOCK:cols] * from_east,
        ]

    for r in range(rows):
        left, right = interior(forced, r)
        field[r, :, 0:BLOCK] = left
        field[r, :, BLOCK:cols] = right
    arrived(fcol_halo, FCOL)
    arrived(prow_halo, PROW)
    columns = spread(fcol_halo)
    order = [0, rows - 1] + list(range(1, rows - 1))
    for place, r in enumerate(order):
        out = with_columns([field[r, :, 0:BLOCK], field[r, :, BLOCK:cols]], r, columns)
        for h in range(halves):
            at = slice(h * BLOCK, (h + 1) * BLOCK)
            if r == 0:
                scale = coef[1, 0:1, at] * tiles_halo[NORTH, 1, rows - 1 : rows, at]
                out[h] = out[h] - scale * prow_halo[0, :, at].astype(F32)
            if r == rows - 1:
                scale = coef[2, r : r + 1, at] * tiles_halo[SOUTH, 1, 0:1, at]
                out[h] = out[h] - scale * prow_halo[1, :, at].astype(F32)
            here = slice(place * probe_count, (place + 1) * probe_count)
            tcat[h, here, 0:BLOCK] = out[h].astype(BF16)
            tcat[h, here, BLOCK : 2 * BLOCK] = out[h].astype(BF16)
    if tokens:
        hear(0)
        for level in range(1, len(tokens)):
            tell(level)

    for d in same_core:
        source = lax.rem(o + n_obs - d, n_obs)
        arrived(wall.at[source], FAR + d // 2 - 1)
        send(wall.at[source], wall.at[source], WALL, sibling)
    arrived(wall.at[pl.ds(0, n_obs // 2)], WALL)
    for i in range(n_obs):
        w_high, w_low = split(wall[i, 0:per_dev, :])
        wcat[i * per_dev : (i + 1) * per_dev, 0:BLOCK] = w_high
        wcat[i * per_dev : (i + 1) * per_dev, BLOCK : 2 * BLOCK] = w_low
    per_row = BLOCK // per_dev
    tails = [wall[i, per_dev : per_dev + 8, :] for i in range(n_obs)]
    chunks = []
    for c in range(obs_total // BLOCK):
        value = tails[c * per_row]
        for k in range(1, per_row):
            value = jnp.where(lane < k * per_dev, value, tails[c * per_row + k])
        chunks.append(value)
    tail = jnp.concatenate(chunks, axis=1)
    obs_at, obs_scale = tail[0:1], tail[1:2]
    weights = wcat[...]
    for group in (order[:2], order[2:]):
        start = order.index(group[0]) * probe_count
        size = len(group) * probe_count
        for h in range(halves):
            picked = dot(tcat[h, start : start + size, :], weights, NT)
            masked = []
            for k, r in enumerate(group):
                own = (r * slab_columns + o * halves + h).astype(F32)
                scale = jnp.where(obs_at == own, obs_scale, 0.0)
                masked.append(picked[k * probe_count : (k + 1) * probe_count] * scale)
            mis_high, mis_low = split(jnp.concatenate(masked, axis=0))
            both = dot(mis_high, weights, NN)
            low = dot(mis_low, weights[:, 0:BLOCK], NN)
            source = both[:, 0:BLOCK] + (both[:, BLOCK:] + low)
            for k, r in enumerate(group):
                field[r, :, h * BLOCK : (h + 1) * BLOCK] = source[
                    k * probe_count : (k + 1) * probe_count
                ]
        if group[0] == 0:
            for i in range(2):
                send(field.at[(rows - 1) * i], srow_halo.at[1 - i], SROW, neighbours[i])
    scol[0] = packed_edges(field, True)
    scol[1] = packed_edges(field, False)
    for i in range(2):
        send(scol.at[i], scol_halo.at[1 - i], SCOL, neighbours[2 + i])

    for r in range(rows):
        left, right = interior(field, r)
        forced[r, :, 0:BLOCK] = left
        forced[r, :, BLOCK:cols] = right
    arrived(scol_halo, SCOL)
    arrived(srow_halo, SROW)
    columns = spread(scol_halo)
    for r in range(rows):
        out = with_columns([forced[r, :, 0:BLOCK], forced[r, :, BLOCK:cols]], r, columns)
        parts = probe_rows(r)
        for h in range(halves):
            at = slice(h * BLOCK, (h + 1) * BLOCK)
            if r == 0:
                out[h] = out[h] - coef[1, 0:1, at] * srow_halo[0, :, at]
            if r == rows - 1:
                out[h] = out[h] - coef[2, r : r + 1, at] * srow_halo[1, :, at]
            s_high, s_low = split(tiles[1, r : r + 1, at] * out[h] + PRIOR * parts[h])
            here = slice(r * cols + h * BLOCK, r * cols + (h + 1) * BLOCK)
            xcat[0:probe_count, here] = s_high
            xcat[probe_count : 2 * probe_count, here] = s_low

    sketch = xcat[...]
    quad = dot(sketch, sketch, NT)
    pair = quad[0:probe_count] + quad[probe_count:]
    gram = pair + shifted(pair, probe_count)
    half = probe_count // 2
    packed = jnp.where(lane < probe_count, gram[0:half], gram[half:])
    for i in range(n_obs):
        part[i] = packed[i * piece : (i + 1) * piece]

    def total(buf, count):
        values = [buf[i] for i in range(count)]
        while len(values) > 1:
            values = [
                sum(values[i : i + 2][1:], values[i]) for i in range(0, len(values), 2)
            ]
        return values[0]

    for peer, slot in zip(obs_peers, obs_slots):
        send(part.at[slot], rs_buf.at[o], RS, peer)
    rs_buf[o] = part[o]
    arrived(rs_buf.at[pl.ds(0, n_obs - 1)], RS)
    y_buf[y] = total(rs_buf, n_obs)
    for peer in y_peers:
        send(y_buf.at[y], y_buf.at[y], YS, peer)
    if tokens:
        for level in range(1, len(tokens)):
            hear(level)
    arrived(y_buf.at[pl.ds(0, ny - 1)], YS)
    z_buf[z] = total(y_buf, ny)
    for d in range(nz // 2, 0, -1):
        send(z_buf.at[z], z_buf.at[z], ZS, z_peer(d))
        if 2 * d < nz:
            send(z_buf.at[z], z_buf.at[z], ZS, z_peer(nz - d))
    arrived(z_buf.at[pl.ds(0, nz - 1)], ZS)
    cells = rows * cols * n_mesh * n_obs
    ag_buf[o] = total(z_buf, nz) / cells
    for peer in obs_peers:
        send(ag_buf.at[o], ag_buf.at[o], AG, peer)
    arrived(ag_buf.at[pl.ds(0, n_obs - 1)], AG)
    for i in range(n_obs):
        gram_ref[i * piece : (i + 1) * piece, :] = ag_buf[i]
    for copy in unsent:
        copy.wait_send()


def eliminate(work, probe_count):
    sub = lax.broadcasted_iota(jnp.int32, (8, BLOCK), 0)
    lanes = lax.broadcasted_iota(jnp.int32, (8, BLOCK), 1)
    groups = len(work)
    factor = [jnp.zeros((8, BLOCK), F32)] * groups
    inverse = [jnp.zeros((8, BLOCK), F32)] * groups

    def wide(x):
        return jnp.broadcast_to(x, (8, BLOCK))

    for k in range(0, probe_count, 4):
        g, s = divmod(k, 8)
        col = [[wide(work[i][:, k + j : k + j + 1]) for i in range(g, groups)] for j in range(4)]
        row = [wide(work[g][s + j : s + j + 1, :]) for j in range(4)]

        def pivot(i, j):
            return wide(col[j][0][s + i : s + i + 1, :])

        a, b, c = pivot(0, 0), pivot(1, 0), pivot(1, 1)
        p, q, t, u = pivot(2, 0), pivot(2, 1), pivot(3, 0), pivot(3, 1)
        det = a * c - b * b
        inv_a, inv_det = 1.0 / a, 1.0 / det
        inv_1 = a * inv_det
        m10 = b * inv_a
        p_0, p_1 = c * p - b * q, a * q - b * p
        t_0, t_1 = c * t - b * u, a * u - b * t
        e = pivot(2, 2) - (p * p_0 + q * p_1) * inv_det
        f = pivot(3, 2) - (t * p_0 + u * p_1) * inv_det
        h = pivot(3, 3) - (t * t_0 + u * t_1) * inv_det
        det_2 = e * h - f * f
        inv_e, inv_det_2 = 1.0 / e, 1.0 / det_2
        inv_3 = e * inv_det_2
        m20, m30 = p * inv_a, t * inv_a
        m21, m31 = (q - m10 * p) * inv_1, (u - m10 * t) * inv_1
        m32 = f * inv_e

        def reduce(v):
            v1 = v[1] - m10 * v[0]
            v2 = v[2] - m20 * v[0] - m21 * v1
            v3 = v[3] - m30 * v[0] - m31 * v1 - m32 * v2
            return v[0], v1, v2, v3

        inv = (inv_a, inv_1, inv_e, inv_3)
        roots = [lax.rsqrt(v) for v in (a, det * inv_a, e, det_2 * inv_e)]
        reduced = reduce(row)
        scaled = [v * w for v, w in zip(reduced, inv)]
        for j in range(4):
            inverse[g] = jnp.where(sub == s + j, reduced[j] * roots[j], inverse[g])
        for i in range(g, groups):
            column = reduce([col[j][i - g] for j in range(4)])
            update = (work[i] - column[0] * scaled[0] - column[1] * scaled[1]) - (
                column[2] * scaled[2] + column[3] * scaled[3]
            )
            for j in range(4):
                keep = column[j] * roots[j]
                if i == g:
                    keep = jnp.where(sub >= s + j, keep, 0.0)
                factor[i] = jnp.where(lanes == k + j, keep, factor[i])
            work[i] = jnp.where(sub > s + 3, update, work[i]) if i == g else update
    return factor, inverse


def basis_kernel(gram_ref, xcat, rank_ref, basis_ref, factor_ref, rows_out):
    probe_count, rows, cols = basis_ref.shape
    halves = cols // BLOCK
    half = probe_count // 2
    groups = probe_count // 8
    sub = lax.broadcasted_iota(jnp.int32, (8, BLOCK), 0)
    lanes = lax.broadcasted_iota(jnp.int32, (8, BLOCK), 1)
    work = []
    for g in range(groups):
        at = 8 * g % half
        own = gram_ref[at : at + 8, :]
        if 8 * g >= half:
            own = shifted(own, probe_count)
        unit = jnp.where(lanes == sub + (8 * g + probe_count), 1.0, 0.0)
        work.append(jnp.where(lanes < probe_count, own, unit))
    factor, inverse = eliminate(work, probe_count)
    rank = rank_ref[0]
    for g in range(groups):
        factor_ref[8 * g : 8 * g + 8, :] = factor[g][:, 0:probe_count]
    lower = jnp.concatenate(
        [
            jnp.where((sub + 8 * g < rank) & (lanes >= probe_count), inverse[g], 0.0)
            for g in range(groups)
        ],
        axis=0,
    )
    lower = lower + shifted(lower, probe_count)
    l_high, l_low = split(lower)
    both = jnp.concatenate([l_high, l_low], axis=0)
    for r in range(rows):
        for h in range(halves):
            here = slice(r * cols + h * BLOCK, r * cols + (h + 1) * BLOCK)
            solved = dot(both, xcat[:, here], NN)
            rows_out[h, pl.ds(r, probe_count, stride=rows), :] = (
                solved[0:probe_count] + solved[probe_count:]
            )
    for h in range(halves):
        basis_ref[:, :, h * BLOCK : (h + 1) * BLOCK] = rows_out[h].reshape(
            probe_count, rows, BLOCK
        )


def per_device(
    n_mesh, n_obs, nz, probes, velocity, viscosity, friction, obs_block, obs_weight, obs_prec, rank
):
    probe_count, rows, cols = probes.shape
    per_dev = obs_weight.shape[1]
    ny = n_mesh // nz
    piece = probe_count // 2 // n_obs
    dma = pltpu.SemaphoreType.DMA
    vmem = pl.BlockSpec(memory_space=pltpu.VMEM)
    xcat, gram = pl.pallas_call(
        functools.partial(sketch_kernel, n_mesh, n_obs, nz),
        out_shape=(
            jax.ShapeDtypeStruct((2 * probe_count, rows * cols), BF16),
            jax.ShapeDtypeStruct((probe_count // 2, BLOCK), F32),
        ),
        in_specs=[pl.BlockSpec(memory_space=pl.ANY)] * 7,
        out_specs=(vmem, vmem),
        scratch_shapes=[
            pltpu.VMEM((probe_count, rows, cols), BF16),
            pltpu.VMEM((rows, cols), F32),
            pltpu.VMEM((1, per_dev), jnp.int32),
            pltpu.VMEM((1, per_dev, BLOCK), F32),
            pltpu.VMEM((1, per_dev), F32),
            pltpu.VMEM((cols // BLOCK, probe_count * rows, BLOCK), F32),
            pltpu.VMEM((rows, probe_count, cols), F32),
            pltpu.VMEM((rows, probe_count, cols), F32),
            pltpu.VMEM((7, rows, cols), F32),
            pltpu.VMEM((2, rows, cols), F32),
            pltpu.VMEM((4, 2, rows, cols), F32),
            pltpu.VMEM((2, probe_count, cols), BF16),
            pltpu.VMEM((2, probe_count, cols), BF16),
            pltpu.VMEM((2, 8, BLOCK), F32),
            pltpu.VMEM((2, 8, BLOCK), F32),
            pltpu.VMEM((2, probe_count, cols), F32),
            pltpu.VMEM((2, 8, BLOCK), F32),
            pltpu.VMEM((2, 8, BLOCK), F32),
            pltpu.VMEM((n_obs, per_dev + 8, BLOCK), F32),
            pltpu.VMEM((n_obs * per_dev, 2 * BLOCK), BF16),
            pltpu.VMEM((cols // BLOCK, rows * probe_count, 2 * BLOCK), BF16),
            pltpu.VMEM((n_obs, piece, BLOCK), F32),
            pltpu.VMEM((n_obs, piece, BLOCK), F32),
            pltpu.VMEM((ny, piece, BLOCK), F32),
            pltpu.VMEM((nz, piece, BLOCK), F32),
            pltpu.VMEM((n_obs, piece, BLOCK), F32),
            dma((7,)),
            dma((10 + n_obs // 2 - 1,)),
            dma((10 + n_obs // 2 - 1,)),
            pltpu.SemaphoreType.REGULAR((2, 2)),
        ],
        compiler_params=pltpu.CompilerParams(collective_id=0, has_side_effects=True),
    )(probes, velocity, viscosity, friction, obs_block, obs_weight, obs_prec)
    basis, factor = pl.pallas_call(
        basis_kernel,
        out_shape=(
            jax.ShapeDtypeStruct((probe_count, rows, cols), F32),
            jax.ShapeDtypeStruct((probe_count, probe_count), F32),
        ),
        in_specs=[vmem, vmem, pl.BlockSpec(memory_space=pltpu.SMEM)],
        out_specs=(vmem, vmem),
        scratch_shapes=[pltpu.VMEM((cols // BLOCK, probe_count * rows, BLOCK), F32)],
    )(gram, xcat, rank)
    return basis, factor


def solution(mesh):
    in_specs = (
        P(None, "mesh", "obs"),
        P("mesh", "obs"),
        P("mesh", "obs"),
        P("mesh", "obs"),
        P("mesh", "obs"),
        P("mesh", "obs", None),
        P("mesh", "obs"),
        P(),
    )
    n_mesh, n_obs = mesh.shape["mesh"], mesh.shape["obs"]
    nz = Z_RING if n_mesh % Z_RING == 0 else n_mesh // 2
    return jax.shard_map(
        functools.partial(per_device, n_mesh, n_obs, nz),
        mesh=mesh,
        in_specs=in_specs,
        out_specs=(P(None, "mesh", "obs"), P()),
        check_vma=False,
    )
```

time: 58.5 us -> 49.7 us (0.85)
  Pallas kernels: 54.5 us -> 48.2 us
  local copies, waits for them, and re-layouts: 2.49 us -> 0 us
    pallas_call x1 -> x2, Pallas kernels: 54.5 us -> 48.2 us  [the longest x1 43.6 us: per_device(): pl.pallas_call(functools.partial(sketch_kernel, n_mesh, n_obs, nz), out_s...]
    unnamed x4 -> x0, local copies, waits for them, and re-layouts: 2.49 us -> none
where the time goes in v2:
time: 49.7 us; the launch traced here: 49.5 us
  Pallas kernels  48.2 us (97%)
  between operations  1.29 us (3%)
    pallas_call x1, Pallas kernels, per_device(): pl.pallas_call(functools.partial(sketch_kernel, n_mesh, n_obs, nz), out_s...  43.6 us
    pallas_call x1, Pallas kernels, per_device(): pl.pallas_call(basis_kernel, out_shape=(jax.ShapeDtypeStruct((probe_count...  4.59 us

profile of v2, /device:TPU:1, one launch (start us, length us, event | category | flops | bytes accessed | tf_op | source)
XLA Modules:
  0.0 49.5 jit_solution(10035920986247837167)
XLA Ops:
  1.3 43.6 %shard_map.95 = (bf16[128,2048]{1,0:T(8,128)(2,1)}, f32[32,128]{1,0:T(8,128)}) custom-call(bf16[64,8,256]{2,1,0:T(8,128)(2,1)} %probes_hbm.1, f32[8,256]{1,0:T(8,128)} %vel_hbm.1, f32[8,256]{1,0:T(8,128)} %visc_hbm.1, f32[8,256]{1,0:T(8,128)} %fric_hbm.1, s32[1,64]{1,0:T(1,128)} %block_hbm.1, f32[1,64,128]{2,1,0:T(8,128)} %weight_hbm.1, f32[1,64]{1,0:T(1,128)} %prec_hbm.1), custom_call_target="tpu_custom_call" | custom-call | tf_op jit(solution)/shard_map/pallas_call | solution.py:539
  44.9 4.6 %shard_map.96 = (f32[64,8,256]{2,1,0:T(8,128)}, f32[64,64]{1,0:T(8,128)}) custom-call(f32[32,128]{1,0:T(8,128)} %get-tuple-element.4.gram_ref, bf16[128,2048]{1,0:T(8,128)(2,1)} %get-tuple-element.5.xcat, s32[1]{0:T(128)S(6)} %copy.10.rank_ref), custom_call_target="tpu_custom_call" | custom-call | tf_op jit(solution)/shard_map/pallas_call | solution.py:581

commit v3 on v2

--- a/solution.py
+++ b/solution.py
@@ -11,6 +11,8 @@
 PRIOR = 1.0
 Z_RING = 16
 NEAR = 2
+WEIGHT_STEPS = 65534.0
+PREC_STEPS = 32768.0
 MESH = pl.DeviceIdType.MESH
 F32 = jnp.float32
 BF16 = jnp.bfloat16
@@ -27,6 +29,10 @@
 def split(x):
     high = x.astype(BF16)
     return high, (x - high.astype(F32)).astype(BF16)
+
+
+def fixed(x):
+    return jnp.floor(x + 0.5).astype(jnp.int32).astype(jnp.int16)
 
 
 def shifted(x, amount):
@@ -45,8 +51,8 @@
     block_hbm,
     weight_hbm,
     prec_hbm,
-    xcat,
-    gram_ref,
+    xcat_hbm,
+    gram_hbm,
     probes_ref,
     fric_ref,
     block_ref,
@@ -65,18 +71,21 @@
     srow_halo,
     scol,
     scol_halo,
+    meta,
     wall,
     wcat,
     tcat,
+    xcat,
     part,
-    rs_buf,
-    y_buf,
+    chip_buf,
+    plane_buf,
     z_buf,
-    ag_buf,
+    both_buf,
     load_sem,
     send_sem,
     recv_sem,
-    token,
+    z_token,
+    y_token,
 ):
     ny = n_mesh // nz
     probe_count, rows, cols = probes_ref.shape
@@ -85,27 +94,40 @@
     per_dev = weight_ref.shape[1]
     obs_total = per_dev * n_obs
     piece = part.shape[1]
+    nx = n_obs // 2
     groups = probe_count // 8
-    TILES, PROW, FCOL, SROW, SCOL, WALL, RS, YS, ZS, AG, FAR = range(11)
+    TILES, PROW, FCOL, SROW, SCOL, WALL, CHIP, PLANE, ZS, BOTH = range(10)
 
     m = lax.axis_index("mesh")
     o = lax.axis_index("obs")
     y = m // nz
     z = lax.rem(m, nz)
+    x = o // 2
+    core = lax.rem(o, 2)
+    sibling = {"obs": o + 1 - 2 * core}
     neighbours = (
         {"mesh": lax.rem(m + n_mesh - 1, n_mesh)},
         {"mesh": lax.rem(m + 1, n_mesh)},
         {"obs": lax.rem(o + n_obs - 1, n_obs)},
         {"obs": lax.rem(o + 1, n_obs)},
     )
-    obs_peers = [{"obs": lax.rem(o + d, n_obs)} for d in range(1, n_obs)]
-    obs_slots = [lax.rem(o + d, n_obs) for d in range(1, n_obs)]
+    obs_peers = [
+        {"obs": lax.rem(o + d, n_obs)}
+        for d in sorted(range(1, n_obs), key=lambda d: -min(d, n_obs - d))
+    ]
+    plane_peers = [
+        {"mesh": lax.rem(y + dy, ny) * nz + z, "obs": lax.rem(o + 2 * dx, n_obs)}
+        for dx, dy in sorted(
+            ((dx, dy) for dx in range(nx) for dy in range(ny) if dx or dy),
+            key=lambda d: -min(d[0], nx - d[0]) - min(d[1], ny - d[1]),
+        )
+    ]
     y_peers = [{"mesh": lax.rem(y + d, ny) * nz + z} for d in range(1, ny)]
 
     def z_peer(d):
         return {"mesh": y * nz + lax.rem(z + d, nz)}
 
-    z_peers = [z_peer(d) for d in range(1, nz)]
+    z_peers = [z_peer(d) for d in sorted(range(1, nz), key=lambda d: -min(d, nz - d))]
     near_z = [z_peer(d) for d in range(1, nz) if min(d, nz - d) <= NEAR]
 
     names = (probes_hbm, weight_hbm, block_hbm, prec_hbm, visc_hbm, vel_hbm, fric_hbm)
@@ -123,14 +145,17 @@
         pl.semaphore_signal(barrier, inc=1, device_id=peer, device_id_type=MESH)
 
     lane = lax.broadcasted_iota(jnp.int32, (1, BLOCK), 1)
-    wall[o, per_dev : per_dev + 8, :] = jnp.zeros((8, BLOCK), F32)
+    meta[...] = jnp.zeros((16, BLOCK), F32)
     for load in loads[1:4]:
         load.wait()
-    wall[o, 0:per_dev, :] = weight_ref[0]
-    wall[o, per_dev : per_dev + 1, 0:per_dev] = block_ref[...].astype(F32)
-    wall[o, per_dev + 1 : per_dev + 2, 0:per_dev] = prec_ref[...]
-    tail = wall[o, per_dev : per_dev + 8, :]
-    wall[o, per_dev : per_dev + 8, :] = tail + shifted(tail, per_dev)
+    wall[o, 0:per_dev, :] = fixed(weight_ref[0] * WEIGHT_STEPS)
+    scaled_prec = prec_ref[...] * PREC_STEPS
+    coarse = jnp.floor(scaled_prec)
+    meta[0:1, 0:per_dev] = block_ref[...].astype(F32)
+    meta[1:2, 0:per_dev] = coarse
+    meta[2:3, 0:per_dev] = (scaled_prec - coarse) * (PREC_STEPS - 1)
+    tail = meta[...]
+    wall[o, per_dev : per_dev + 16, :] = fixed(tail + shifted(tail, per_dev))
 
     loads[0].wait()
     for h in range(halves):
@@ -205,11 +230,8 @@
         send(fcol.at[i], fcol_halo.at[1 - i], FCOL, neighbours[2 + i])
     for i in range(2):
         send(prow.at[i], prow_halo.at[1 - i], PROW, neighbours[i])
-    sibling = {"obs": o + 1 - 2 * lax.rem(o, 2)}
-    same_core = sorted(range(2, n_obs, 2), key=lambda d: min(d, n_obs - d))
-    for d in same_core:
-        send(wall.at[o], wall.at[o], FAR + d // 2 - 1, {"obs": lax.rem(o + d, n_obs)})
-    send(wall.at[o], wall.at[o], WALL, sibling)
+    for peer in obs_peers:
+        send(wall.at[o], wall.at[o], WALL, peer)
 
     tokens = []
     reach = NEAR
@@ -220,13 +242,17 @@
     def tell(level):
         for side, d in enumerate((tokens[level], nz - tokens[level])):
             pl.semaphore_signal(
-                token.at[level, side], inc=1, device_id=z_peer(d), device_id_type=MESH
+                z_token.at[level, side], inc=1, device_id=z_peer(d), device_id_type=MESH
             )
 
     def hear(level):
         for side in range(2):
-            pl.semaphore_wait(token.at[level, side], 1)
-
+            pl.semaphore_wait(z_token.at[level, side], 1)
+
+    for d in range(1, ny):
+        pl.semaphore_signal(
+            y_token.at[d - 1], inc=1, device_id=y_peers[d - 1], device_id_type=MESH
+        )
     if tokens:
         tell(0)
 
@@ -311,17 +337,13 @@
         for level in range(1, len(tokens)):
             tell(level)
 
-    for d in same_core:
-        source = lax.rem(o + n_obs - d, n_obs)
-        arrived(wall.at[source], FAR + d // 2 - 1)
-        send(wall.at[source], wall.at[source], WALL, sibling)
-    arrived(wall.at[pl.ds(0, n_obs // 2)], WALL)
+    arrived(wall.at[pl.ds(0, n_obs - 1)], WALL)
     for i in range(n_obs):
-        w_high, w_low = split(wall[i, 0:per_dev, :])
+        w_high, w_low = split(wall[i, 0:per_dev, :].astype(jnp.int32).astype(F32))
         wcat[i * per_dev : (i + 1) * per_dev, 0:BLOCK] = w_high
         wcat[i * per_dev : (i + 1) * per_dev, BLOCK : 2 * BLOCK] = w_low
     per_row = BLOCK // per_dev
-    tails = [wall[i, per_dev : per_dev + 8, :] for i in range(n_obs)]
+    tails = [wall[i, per_dev : per_dev + 16, :].astype(jnp.int32).astype(F32) for i in range(n_obs)]
     chunks = []
     for c in range(obs_total // BLOCK):
         value = tails[c * per_row]
@@ -329,7 +351,9 @@
             value = jnp.where(lane < k * per_dev, value, tails[c * per_row + k])
         chunks.append(value)
     tail = jnp.concatenate(chunks, axis=1)
-    obs_at, obs_scale = tail[0:1], tail[1:2]
+    obs_at = tail[0:1]
+    prec = (tail[1:2] + tail[2:3] * (1.0 / (PREC_STEPS - 1))) * (1.0 / PREC_STEPS)
+    obs_scale = prec * (1.0 / WEIGHT_STEPS**2)
     weights = wcat[...]
     for group in (order[:2], order[2:]):
         start = order.index(group[0]) * probe_count
@@ -362,29 +386,39 @@
         forced[r, :, 0:BLOCK] = left
         forced[r, :, BLOCK:cols] = right
     arrived(scol_halo, SCOL)
-    arrived(srow_halo, SROW)
     columns = spread(scol_halo)
-    for r in range(rows):
-        out = with_columns([forced[r, :, 0:BLOCK], forced[r, :, BLOCK:cols]], r, columns)
-        parts = probe_rows(r)
-        for h in range(halves):
-            at = slice(h * BLOCK, (h + 1) * BLOCK)
-            if r == 0:
-                out[h] = out[h] - coef[1, 0:1, at] * srow_halo[0, :, at]
-            if r == rows - 1:
-                out[h] = out[h] - coef[2, r : r + 1, at] * srow_halo[1, :, at]
-            s_high, s_low = split(tiles[1, r : r + 1, at] * out[h] + PRIOR * parts[h])
-            here = slice(r * cols + h * BLOCK, r * cols + (h + 1) * BLOCK)
-            xcat[0:probe_count, here] = s_high
-            xcat[probe_count : 2 * probe_count, here] = s_low
-
-    sketch = xcat[...]
-    quad = dot(sketch, sketch, NT)
+    quad = 0.0
+    for group in (order[2:], order[:2]):
+        if group[0] == 0:
+            arrived(srow_halo, SROW)
+        for r in group:
+            out = with_columns([forced[r, :, 0:BLOCK], forced[r, :, BLOCK:cols]], r, columns)
+            parts = probe_rows(r)
+            for h in range(halves):
+                at = slice(h * BLOCK, (h + 1) * BLOCK)
+                if r == 0:
+                    out[h] = out[h] - coef[1, 0:1, at] * srow_halo[0, :, at]
+                if r == rows - 1:
+                    out[h] = out[h] - coef[2, r : r + 1, at] * srow_halo[1, :, at]
+                s_high, s_low = split(tiles[1, r : r + 1, at] * out[h] + PRIOR * parts[h])
+                here = slice(r * cols + h * BLOCK, r * cols + (h + 1) * BLOCK)
+                xcat[0:probe_count, here] = s_high
+                xcat[probe_count : 2 * probe_count, here] = s_low
+        if group[0] == 0:
+            both = [xcat[:, r * cols : (r + 1) * cols] for r in group]
+            for sketch in both:
+                quad = quad + dot(sketch, sketch, NT)
+        else:
+            sketch = xcat[:, group[0] * cols : (group[-1] + 1) * cols]
+            quad = dot(sketch, sketch, NT)
+
+    keep_sketch = pltpu.make_async_copy(xcat, xcat_hbm, load_sem.at[0])
+    keep_sketch.start()
     pair = quad[0:probe_count] + quad[probe_count:]
     gram = pair + shifted(pair, probe_count)
     half = probe_count // 2
     packed = jnp.where(lane < probe_count, gram[0:half], gram[half:])
-    for i in range(n_obs):
+    for i in range(2):
         part[i] = packed[i * piece : (i + 1) * piece]
 
     def total(buf, count):
@@ -395,32 +429,32 @@
             ]
         return values[0]
 
-    for peer, slot in zip(obs_peers, obs_slots):
-        send(part.at[slot], rs_buf.at[o], RS, peer)
-    rs_buf[o] = part[o]
-    arrived(rs_buf.at[pl.ds(0, n_obs - 1)], RS)
-    y_buf[y] = total(rs_buf, n_obs)
-    for peer in y_peers:
-        send(y_buf.at[y], y_buf.at[y], YS, peer)
+    send(part.at[1 - core], chip_buf, CHIP, sibling)
+    for d in range(1, ny):
+        pl.semaphore_wait(y_token.at[d - 1], 1)
+    arrived(chip_buf, CHIP)
+    here = y * nx + x
+    plane_buf[here] = part[core] + chip_buf[...]
+    for peer in plane_peers:
+        send(plane_buf.at[here], plane_buf.at[here], PLANE, peer)
     if tokens:
         for level in range(1, len(tokens)):
             hear(level)
-    arrived(y_buf.at[pl.ds(0, ny - 1)], YS)
-    z_buf[z] = total(y_buf, ny)
-    for d in range(nz // 2, 0, -1):
-        send(z_buf.at[z], z_buf.at[z], ZS, z_peer(d))
-        if 2 * d < nz:
-            send(z_buf.at[z], z_buf.at[z], ZS, z_peer(nz - d))
+    arrived(plane_buf.at[pl.ds(0, nx * ny - 1)], PLANE)
+    z_buf[z] = total(plane_buf, nx * ny)
+    for peer in z_peers:
+        send(z_buf.at[z], z_buf.at[z], ZS, peer)
     arrived(z_buf.at[pl.ds(0, nz - 1)], ZS)
     cells = rows * cols * n_mesh * n_obs
-    ag_buf[o] = total(z_buf, nz) / cells
-    for peer in obs_peers:
-        send(ag_buf.at[o], ag_buf.at[o], AG, peer)
-    arrived(ag_buf.at[pl.ds(0, n_obs - 1)], AG)
-    for i in range(n_obs):
-        gram_ref[i * piece : (i + 1) * piece, :] = ag_buf[i]
+    both_buf[core] = total(z_buf, nz) / cells
+    send(both_buf.at[core], both_buf.at[core], BOTH, sibling)
+    arrived(both_buf.at[0], BOTH)
+    keep_gram = pltpu.make_async_copy(both_buf, gram_hbm, load_sem.at[1])
+    keep_gram.start()
     for copy in unsent:
         copy.wait_send()
+    keep_sketch.wait()
+    keep_gram.wait()
 
 
 def eliminate(work, probe_count):
@@ -485,18 +519,25 @@
     return factor, inverse
 
 
-def basis_kernel(gram_ref, xcat, rank_ref, basis_ref, factor_ref, rows_out):
-    probe_count, rows, cols = basis_ref.shape
-    halves = cols // BLOCK
-    half = probe_count // 2
+def basis_kernel(gram_hbm, xcat_hbm, rank_ref, basis_hbm, factor_ref, gram_ref, xcat, out, sem):
+    halves, cells, _ = out.shape
+    probe_count = factor_ref.shape[0]
+    rows = cells // probe_count
+    cols = halves * BLOCK
+    piece = gram_ref.shape[1]
     groups = probe_count // 8
+    load_gram = pltpu.make_async_copy(gram_hbm, gram_ref, sem.at[0])
+    load_gram.start()
+    load_sketch = pltpu.make_async_copy(xcat_hbm, xcat, sem.at[1])
+    load_sketch.start()
+    load_gram.wait()
     sub = lax.broadcasted_iota(jnp.int32, (8, BLOCK), 0)
     lanes = lax.broadcasted_iota(jnp.int32, (8, BLOCK), 1)
     work = []
     for g in range(groups):
-        at = 8 * g % half
-        own = gram_ref[at : at + 8, :]
-        if 8 * g >= half:
+        at = 8 * g % piece
+        own = gram_ref[8 * g // piece % 2, at : at + 8, :]
+        if 8 * g >= 2 * piece:
             own = shifted(own, probe_count)
         unit = jnp.where(lanes == sub + (8 * g + probe_count), 1.0, 0.0)
         work.append(jnp.where(lanes < probe_count, own, unit))
@@ -514,17 +555,22 @@
     lower = lower + shifted(lower, probe_count)
     l_high, l_low = split(lower)
     both = jnp.concatenate([l_high, l_low], axis=0)
-    for r in range(rows):
-        for h in range(halves):
+    load_sketch.wait()
+    stores = []
+    for h in range(halves):
+        for r in range(rows):
             here = slice(r * cols + h * BLOCK, r * cols + (h + 1) * BLOCK)
             solved = dot(both, xcat[:, here], NN)
-            rows_out[h, pl.ds(r, probe_count, stride=rows), :] = (
+            out[h, pl.ds(r, probe_count, stride=rows), :] = (
                 solved[0:probe_count] + solved[probe_count:]
             )
-    for h in range(halves):
-        basis_ref[:, :, h * BLOCK : (h + 1) * BLOCK] = rows_out[h].reshape(
-            probe_count, rows, BLOCK
+        store = pltpu.make_async_copy(
+            out.at[h], basis_hbm.at[:, pl.ds(h * BLOCK, BLOCK)], sem.at[2 + h]
         )
+        store.start()
+        stores.append(store)
+    for store in stores:
+        store.wait()
 
 
 def per_device(
@@ -533,17 +579,18 @@
     probe_count, rows, cols = probes.shape
     per_dev = obs_weight.shape[1]
     ny = n_mesh // nz
-    piece = probe_count // 2 // n_obs
+    piece = probe_count // 4
     dma = pltpu.SemaphoreType.DMA
     vmem = pl.BlockSpec(memory_space=pltpu.VMEM)
+    hbm = pl.BlockSpec(memory_space=pltpu.HBM)
     xcat, gram = pl.pallas_call(
         functools.partial(sketch_kernel, n_mesh, n_obs, nz),
         out_shape=(
             jax.ShapeDtypeStruct((2 * probe_count, rows * cols), BF16),
-            jax.ShapeDtypeStruct((probe_count // 2, BLOCK), F32),
+            jax.ShapeDtypeStruct((2, piece, BLOCK), F32),
         ),
-        in_specs=[pl.BlockSpec(memory_space=pl.ANY)] * 7,
-        out_specs=(vmem, vmem),
+        in_specs=[hbm] * 7,
+        out_specs=(hbm, hbm),
         scratch_shapes=[
             pltpu.VMEM((probe_count, rows, cols), BF16),
             pltpu.VMEM((rows, cols), F32),
@@ -563,32 +610,40 @@
             pltpu.VMEM((2, probe_count, cols), F32),
             pltpu.VMEM((2, 8, BLOCK), F32),
             pltpu.VMEM((2, 8, BLOCK), F32),
-            pltpu.VMEM((n_obs, per_dev + 8, BLOCK), F32),
+            pltpu.VMEM((16, BLOCK), F32),
+            pltpu.VMEM((n_obs, per_dev + 16, BLOCK), jnp.int16),
             pltpu.VMEM((n_obs * per_dev, 2 * BLOCK), BF16),
             pltpu.VMEM((cols // BLOCK, rows * probe_count, 2 * BLOCK), BF16),
-            pltpu.VMEM((n_obs, piece, BLOCK), F32),
-            pltpu.VMEM((n_obs, piece, BLOCK), F32),
-            pltpu.VMEM((ny, piece, BLOCK), F32),
+            pltpu.VMEM((2 * probe_count, rows * cols), BF16),
+            pltpu.VMEM((2, piece, BLOCK), F32),
+            pltpu.VMEM((piece, BLOCK), F32),
+            pltpu.VMEM((n_obs // 2 * ny, piece, BLOCK), F32),
             pltpu.VMEM((nz, piece, BLOCK), F32),
-            pltpu.VMEM((n_obs, piece, BLOCK), F32),
+            pltpu.VMEM((2, piece, BLOCK), F32),
             dma((7,)),
-            dma((10 + n_obs // 2 - 1,)),
-            dma((10 + n_obs // 2 - 1,)),
+            dma((10,)),
+            dma((10,)),
             pltpu.SemaphoreType.REGULAR((2, 2)),
+            pltpu.SemaphoreType.REGULAR((max(ny - 1, 1),)),
         ],
         compiler_params=pltpu.CompilerParams(collective_id=0, has_side_effects=True),
     )(probes, velocity, viscosity, friction, obs_block, obs_weight, obs_prec)
     basis, factor = pl.pallas_call(
         basis_kernel,
         out_shape=(
-            jax.ShapeDtypeStruct((probe_count, rows, cols), F32),
+            jax.ShapeDtypeStruct((probe_count * rows, cols), F32),
             jax.ShapeDtypeStruct((probe_count, probe_count), F32),
         ),
-        in_specs=[vmem, vmem, pl.BlockSpec(memory_space=pltpu.SMEM)],
-        out_specs=(vmem, vmem),
-        scratch_shapes=[pltpu.VMEM((cols // BLOCK, probe_count * rows, BLOCK), F32)],
+        in_specs=[hbm, hbm, pl.BlockSpec(memory_space=pltpu.SMEM)],
+        out_specs=(hbm, vmem),
+        scratch_shapes=[
+            pltpu.VMEM((2, piece, BLOCK), F32),
+            pltpu.VMEM((2 * probe_count, rows * cols), BF16),
+            pltpu.VMEM((cols // BLOCK, probe_count * rows, BLOCK), F32),
+            dma((2 + cols // BLOCK,)),
+        ],
     )(gram, xcat, rank)
-    return basis, factor
+    return basis.reshape(probe_count, rows, cols), factor
 
 
 def solution(mesh):

time: 49.7 us -> 46.1 us (0.928)
  Pallas kernels: 48.2 us -> 44.6 us
    pallas_call x1, Pallas kernels: 43.6 us -> 39.8 us  [per_device(): pl.pallas_call(functools.partial(sketch_kernel, n_mesh, n_obs, nz), out_s...]
where the time goes in v3:
time: 46.1 us; the launch traced here: 45.9 us
  Pallas kernels  44.6 us (97%)
  between operations  1.29 us (3%)
    pallas_call x1, Pallas kernels, per_device(): pl.pallas_call(functools.partial(sketch_kernel, n_mesh, n_obs, nz), out_s...  39.8 us
    pallas_call x1, Pallas kernels, per_device(): pl.pallas_call(basis_kernel, out_shape=(jax.ShapeDtypeStruct((probe_count...  4.8 us

profile of v3, /device:TPU:1, one launch (start us, length us, event | category | flops | bytes accessed | tf_op | source)
XLA Modules:
  0.0 45.9 jit_solution(5625096069843192547)
XLA Ops:
  1.3 39.8 %shard_map.95 = (bf16[128,2048]{1,0:T(8,128)(2,1)}, f32[2,16,128]{2,1,0:T(8,128)}) custom-call(bf16[64,8,256]{2,1,0:T(8,128)(2,1)} %probes_hbm.1, f32[8,256]{1,0:T(8,128)} %vel_hbm.1, f32[8,256]{1,0:T(8,128)} %visc_hbm.1, f32[8,256]{1,0:T(8,128)} %fric_hbm.1, s32[1,64]{1,0:T(1,128)} %block_hbm.1, f32[1,64,128]{2,1,0:T(8,128)} %weight_hbm.1, f32[1,64]{1,0:T(1,128)} %prec_hbm.1), custom_call_target="tpu_custom_call" | custom-call | tf_op jit(solution)/shard_map/pallas_call | solution.py:586
  41.1 4.8 %shard_map.96 = (f32[512,256]{1,0:T(8,128)}, f32[64,64]{1,0:T(8,128)}) custom-call(f32[2,16,128]{2,1,0:T(8,128)} %get-tuple-element.6.gram_hbm, bf16[128,2048]{1,0:T(8,128)(2,1)} %get-tuple-element.7.xcat_hbm, s32[1]{0:T(128)S(6)} %copy.10.rank_ref), custom_call_target="tpu_custom_call" | custom-call | tf_op jit(solution)/shard_map/pallas_call | solution.py:631

commit v4 on v3

--- a/solution.py
+++ b/solution.py
@@ -11,6 +11,7 @@
 PRIOR = 1.0
 Z_RING = 16
 NEAR = 2
+PIVOTS = 8
 WEIGHT_STEPS = 65534.0
 PREC_STEPS = 32768.0
 MESH = pl.DeviceIdType.MESH
@@ -96,7 +97,7 @@
     piece = part.shape[1]
     nx = n_obs // 2
     groups = probe_count // 8
-    TILES, PROW, FCOL, SROW, SCOL, WALL, CHIP, PLANE, ZS, BOTH = range(10)
+    WALL, CHIP, PLANE, ZS, BOTH, TILES, FORCED, SOURCE = 0, 1, 2, 3, 4, 5, 9, 13
 
     m = lax.axis_index("mesh")
     o = lax.axis_index("obs")
@@ -140,9 +141,27 @@
         load.start()
 
     barrier = pltpu.get_barrier_semaphore()
-    partners = list(neighbours[:2]) + obs_peers + y_peers + near_z
+    inner = (m > 0, m < n_mesh - 1, o > 0, o < n_obs - 1)
+    over_wrap = (inner[NORTH] & (z == 0), inner[SOUTH] & (z == nz - 1))
+    partners = obs_peers + y_peers + near_z
     for peer in partners:
         pl.semaphore_signal(barrier, inc=1, device_id=peer, device_id_type=MESH)
+    for side in (NORTH, SOUTH):
+
+        @pl.when(over_wrap[side])
+        def _():
+            pl.semaphore_signal(
+                barrier, inc=1, device_id=neighbours[side], device_id_type=MESH
+            )
+
+    rows_in, columns_in = (prow_halo, srow_halo), (fcol_halo, scol_halo)
+    for side in range(4):
+
+        @pl.when(jnp.logical_not(inner[side]))
+        def _():
+            tiles_halo[side] = jnp.zeros((2, rows, cols), F32)
+            for buf in columns_in if side >= WEST else rows_in:
+                buf[side % 2] = jnp.zeros(buf.shape[1:], buf.dtype)
 
     lane = lax.broadcasted_iota(jnp.int32, (1, BLOCK), 1)
     meta[...] = jnp.zeros((16, BLOCK), F32)
@@ -195,7 +214,10 @@
     fcol[0] = packed_edges(forced, True)
     fcol[1] = packed_edges(forced, False)
 
-    pl.semaphore_wait(barrier, len(partners))
+    pl.semaphore_wait(
+        barrier,
+        len(partners) + over_wrap[0].astype(jnp.int32) + over_wrap[1].astype(jnp.int32),
+    )
 
     def send(src, dst, stage, peer):
         pltpu.make_async_remote_copy(
@@ -224,12 +246,35 @@
         unsent.append(copy)
         copy.wait_recv()
 
+    edge_copies = []
+
+    def to_neighbour(src, dst, stage, side):
+        there = OPPOSITE[side]
+
+        @pl.when(inner[side])
+        def _():
+            pltpu.make_async_remote_copy(
+                src_ref=src,
+                dst_ref=dst,
+                send_sem=send_sem.at[stage + side],
+                recv_sem=recv_sem.at[stage + there],
+                device_id=neighbours[side],
+                device_id_type=MESH,
+            ).start()
+
+        edge_copies.append((src, stage + side, side))
+
+    def from_neighbour(buf, stage, side):
+        @pl.when(inner[side])
+        def _():
+            whole(buf, stage + side).wait_recv()
+
     for side in range(4):
-        send(tiles, tiles_halo.at[OPPOSITE[side]], TILES, neighbours[side])
+        to_neighbour(tiles, tiles_halo.at[OPPOSITE[side]], TILES, side)
     for i in range(2):
-        send(fcol.at[i], fcol_halo.at[1 - i], FCOL, neighbours[2 + i])
+        to_neighbour(fcol.at[i], fcol_halo.at[1 - i], FORCED, WEST + i)
     for i in range(2):
-        send(prow.at[i], prow_halo.at[1 - i], PROW, neighbours[i])
+        to_neighbour(prow.at[i], prow_halo.at[1 - i], FORCED, NORTH + i)
     for peer in obs_peers:
         send(wall.at[o], wall.at[o], WALL, peer)
 
@@ -256,10 +301,10 @@
     if tokens:
         tell(0)
 
-    arrived(tiles_halo, TILES)
+    for side in range(4):
+        from_neighbour(tiles_halo.at[side], TILES, side)
     row_id = lax.broadcasted_iota(jnp.int32, (rows, cols), 0)
     col_id = lax.broadcasted_iota(jnp.int32, (rows, cols), 1)
-    inner = (m > 0, m < n_mesh - 1, o > 0, o < n_obs - 1)
     visc = tiles[0]
 
     def face(side, shift, axis, edge):
@@ -315,12 +360,15 @@
         left, right = interior(forced, r)
         field[r, :, 0:BLOCK] = left
         field[r, :, BLOCK:cols] = right
-    arrived(fcol_halo, FCOL)
-    arrived(prow_halo, PROW)
+    for i in range(2):
+        from_neighbour(fcol_halo.at[i], FORCED, WEST + i)
     columns = spread(fcol_halo)
     order = [0, rows - 1] + list(range(1, rows - 1))
-    for place, r in enumerate(order):
+
+    def tangent(r):
         out = with_columns([field[r, :, 0:BLOCK], field[r, :, BLOCK:cols]], r, columns)
+        place = order.index(r)
+        here = slice(place * probe_count, (place + 1) * probe_count)
         for h in range(halves):
             at = slice(h * BLOCK, (h + 1) * BLOCK)
             if r == 0:
@@ -329,9 +377,11 @@
             if r == rows - 1:
                 scale = coef[2, r : r + 1, at] * tiles_halo[SOUTH, 1, 0:1, at]
                 out[h] = out[h] - scale * prow_halo[1, :, at].astype(F32)
-            here = slice(place * probe_count, (place + 1) * probe_count)
             tcat[h, here, 0:BLOCK] = out[h].astype(BF16)
             tcat[h, here, BLOCK : 2 * BLOCK] = out[h].astype(BF16)
+
+    for r in order[2:]:
+        tangent(r)
     if tokens:
         hear(0)
         for level in range(1, len(tokens)):
@@ -355,6 +405,10 @@
     prec = (tail[1:2] + tail[2:3] * (1.0 / (PREC_STEPS - 1))) * (1.0 / PREC_STEPS)
     obs_scale = prec * (1.0 / WEIGHT_STEPS**2)
     weights = wcat[...]
+    for i in range(2):
+        from_neighbour(prow_halo.at[i], FORCED, NORTH + i)
+    for r in order[:2]:
+        tangent(r)
     for group in (order[:2], order[2:]):
         start = order.index(group[0]) * probe_count
         size = len(group) * probe_count
@@ -375,22 +429,24 @@
                 ]
         if group[0] == 0:
             for i in range(2):
-                send(field.at[(rows - 1) * i], srow_halo.at[1 - i], SROW, neighbours[i])
+                to_neighbour(field.at[(rows - 1) * i], srow_halo.at[1 - i], SOURCE, NORTH + i)
     scol[0] = packed_edges(field, True)
     scol[1] = packed_edges(field, False)
     for i in range(2):
-        send(scol.at[i], scol_halo.at[1 - i], SCOL, neighbours[2 + i])
+        to_neighbour(scol.at[i], scol_halo.at[1 - i], SOURCE, WEST + i)
 
     for r in range(rows):
         left, right = interior(field, r)
         forced[r, :, 0:BLOCK] = left
         forced[r, :, BLOCK:cols] = right
-    arrived(scol_halo, SCOL)
+    for i in range(2):
+        from_neighbour(scol_halo.at[i], SOURCE, WEST + i)
     columns = spread(scol_halo)
     quad = 0.0
     for group in (order[2:], order[:2]):
         if group[0] == 0:
-            arrived(srow_halo, SROW)
+            for i in range(2):
+                from_neighbour(srow_halo.at[i], SOURCE, NORTH + i)
         for r in group:
             out = with_columns([forced[r, :, 0:BLOCK], forced[r, :, BLOCK:cols]], r, columns)
             parts = probe_rows(r)
@@ -453,6 +509,12 @@
     keep_gram.start()
     for copy in unsent:
         copy.wait_send()
+    for src, at, side in edge_copies:
+
+        @pl.when(inner[side])
+        def _():
+            whole(src, at).wait_send()
+
     keep_sketch.wait()
     keep_gram.wait()
 
@@ -467,59 +529,64 @@
     def wide(x):
         return jnp.broadcast_to(x, (8, BLOCK))
 
-    for k in range(0, probe_count, 4):
+    for k in range(0, probe_count, PIVOTS):
         g, s = divmod(k, 8)
-        col = [[wide(work[i][:, k + j : k + j + 1]) for i in range(g, groups)] for j in range(4)]
-        row = [wide(work[g][s + j : s + j + 1, :]) for j in range(4)]
-
-        def pivot(i, j):
-            return wide(col[j][0][s + i : s + i + 1, :])
-
-        a, b, c = pivot(0, 0), pivot(1, 0), pivot(1, 1)
-        p, q, t, u = pivot(2, 0), pivot(2, 1), pivot(3, 0), pivot(3, 1)
-        det = a * c - b * b
-        inv_a, inv_det = 1.0 / a, 1.0 / det
-        inv_1 = a * inv_det
-        m10 = b * inv_a
-        p_0, p_1 = c * p - b * q, a * q - b * p
-        t_0, t_1 = c * t - b * u, a * u - b * t
-        e = pivot(2, 2) - (p * p_0 + q * p_1) * inv_det
-        f = pivot(3, 2) - (t * p_0 + u * p_1) * inv_det
-        h = pivot(3, 3) - (t * t_0 + u * t_1) * inv_det
-        det_2 = e * h - f * f
-        inv_e, inv_det_2 = 1.0 / e, 1.0 / det_2
-        inv_3 = e * inv_det_2
-        m20, m30 = p * inv_a, t * inv_a
-        m21, m31 = (q - m10 * p) * inv_1, (u - m10 * t) * inv_1
-        m32 = f * inv_e
+        span = range(PIVOTS)
+        col = [[wide(work[i][:, k + j : k + j + 1]) for i in range(g, groups)] for j in span]
+        row = [wide(work[g][s + j : s + j + 1, :]) for j in span]
+        local = [[wide(col[j][0][s + i : s + i + 1, :]) for j in range(i + 1)] for i in span]
+        lower = [[None] * PIVOTS for _ in span]
+        inv, roots = [], []
+        for p in range(0, PIVOTS, 2):
+            a, b, c = local[p][p], local[p + 1][p], local[p + 1][p + 1]
+            det = a * c - b * b
+            inv_a, inv_det = 1.0 / a, 1.0 / det
+            inv_1 = a * inv_det
+            slope = b * inv_a
+            inv += [inv_a, inv_1]
+            roots += [lax.rsqrt(a), lax.rsqrt(det * inv_a)]
+            lower[p + 1][p] = slope
+            for i in range(p + 2, PIVOTS):
+                u, v = local[i][p], local[i][p + 1]
+                lower[i][p] = u * inv_a
+                lower[i][p + 1] = (v - slope * u) * inv_1
+                for j in range(p + 2, i + 1):
+                    t, w = local[j][p], local[j][p + 1]
+                    local[i][j] = (
+                        local[i][j] - (u * (c * t - b * w) + v * (a * w - b * t)) * inv_det
+                    )
 
         def reduce(v):
-            v1 = v[1] - m10 * v[0]
-            v2 = v[2] - m20 * v[0] - m21 * v1
-            v3 = v[3] - m30 * v[0] - m31 * v1 - m32 * v2
-            return v[0], v1, v2, v3
-
-        inv = (inv_a, inv_1, inv_e, inv_3)
-        roots = [lax.rsqrt(v) for v in (a, det * inv_a, e, det_2 * inv_e)]
+            done = []
+            for j in span:
+                value = v[j]
+                for i in range(j):
+                    value = value - lower[j][i] * done[i]
+                done.append(value)
+            return done
+
         reduced = reduce(row)
         scaled = [v * w for v, w in zip(reduced, inv)]
-        for j in range(4):
+        for j in span:
             inverse[g] = jnp.where(sub == s + j, reduced[j] * roots[j], inverse[g])
         for i in range(g, groups):
-            column = reduce([col[j][i - g] for j in range(4)])
-            update = (work[i] - column[0] * scaled[0] - column[1] * scaled[1]) - (
-                column[2] * scaled[2] + column[3] * scaled[3]
-            )
-            for j in range(4):
+            column = reduce([col[j][i - g] for j in span])
+            if not (i == g and s + PIVOTS == 8):
+                update = work[i]
+                for j in range(0, PIVOTS, 2):
+                    update = update - (column[j] * scaled[j] + column[j + 1] * scaled[j + 1])
+                work[i] = jnp.where(sub >= s + PIVOTS, update, work[i]) if i == g else update
+            for j in span:
                 keep = column[j] * roots[j]
                 if i == g:
                     keep = jnp.where(sub >= s + j, keep, 0.0)
                 factor[i] = jnp.where(lanes == k + j, keep, factor[i])
-            work[i] = jnp.where(sub > s + 3, update, work[i]) if i == g else update
     return factor, inverse
 
 
-def basis_kernel(gram_hbm, xcat_hbm, rank_ref, basis_hbm, factor_ref, gram_ref, xcat, out, sem):
+def basis_kernel(
+    gram_hbm, xcat_hbm, rank_hbm, basis_hbm, factor_ref, gram_ref, xcat, rank_ref, out, sem
+):
     halves, cells, _ = out.shape
     probe_count = factor_ref.shape[0]
     rows = cells // probe_count
@@ -530,6 +597,8 @@
     load_gram.start()
     load_sketch = pltpu.make_async_copy(xcat_hbm, xcat, sem.at[1])
     load_sketch.start()
+    load_rank = pltpu.make_async_copy(rank_hbm, rank_ref, sem.at[2])
+    load_rank.start()
     load_gram.wait()
     sub = lax.broadcasted_iota(jnp.int32, (8, BLOCK), 0)
     lanes = lax.broadcasted_iota(jnp.int32, (8, BLOCK), 1)
@@ -542,6 +611,7 @@
         unit = jnp.where(lanes == sub + (8 * g + probe_count), 1.0, 0.0)
         work.append(jnp.where(lanes < probe_count, own, unit))
     factor, inverse = eliminate(work, probe_count)
+    load_rank.wait()
     rank = rank_ref[0]
     for g in range(groups):
         factor_ref[8 * g : 8 * g + 8, :] = factor[g][:, 0:probe_count]
@@ -565,7 +635,7 @@
                 solved[0:probe_count] + solved[probe_count:]
             )
         store = pltpu.make_async_copy(
-            out.at[h], basis_hbm.at[:, pl.ds(h * BLOCK, BLOCK)], sem.at[2 + h]
+            out.at[h], basis_hbm.at[:, pl.ds(h * BLOCK, BLOCK)], sem.at[3 + h]
         )
         store.start()
         stores.append(store)
@@ -621,8 +691,8 @@
             pltpu.VMEM((nz, piece, BLOCK), F32),
             pltpu.VMEM((2, piece, BLOCK), F32),
             dma((7,)),
-            dma((10,)),
-            dma((10,)),
+            dma((17,)),
+            dma((17,)),
             pltpu.SemaphoreType.REGULAR((2, 2)),
             pltpu.SemaphoreType.REGULAR((max(ny - 1, 1),)),
         ],
@@ -634,13 +704,14 @@
             jax.ShapeDtypeStruct((probe_count * rows, cols), F32),
             jax.ShapeDtypeStruct((probe_count, probe_count), F32),
         ),
-        in_specs=[hbm, hbm, pl.BlockSpec(memory_space=pltpu.SMEM)],
+        in_specs=[hbm, hbm, hbm],
         out_specs=(hbm, vmem),
         scratch_shapes=[
             pltpu.VMEM((2, piece, BLOCK), F32),
             pltpu.VMEM((2 * probe_count, rows * cols), BF16),
+            pltpu.SMEM((1,), jnp.int32),
             pltpu.VMEM((cols // BLOCK, probe_count * rows, BLOCK), F32),
-            dma((2 + cols // BLOCK,)),
+            dma((3 + cols // BLOCK,)),
         ],
     )(gram, xcat, rank)
     return basis.reshape(probe_count, rows, cols), factor

time: 46.1 us -> 46.3 us (level)
    pallas_call x1, Pallas kernels: 39.8 us -> 40.6 us  [per_device(): pl.pallas_call(functools.partial(sketch_kernel, n_mesh, n_obs, nz), out_s...]
    pallas_call x1, Pallas kernels: 4.8 us -> 4.25 us  [per_device(): pl.pallas_call(basis_kernel, out_shape=(jax.ShapeDtypeStruct((probe_count...]
where the time goes in v4:
time: 46.3 us; the launch traced here: 46.1 us
  Pallas kernels  44.8 us (97%)
  between operations  1.29 us (3%)
    pallas_call x1, Pallas kernels, per_device(): pl.pallas_call(functools.partial(sketch_kernel, n_mesh, n_obs, nz), out_s...  40.6 us
    pallas_call x1, Pallas kernels, per_device(): pl.pallas_call(basis_kernel, out_shape=(jax.ShapeDtypeStruct((probe_count...  4.25 us

profile of v4, /device:TPU:1, one launch (start us, length us, event | category | flops | bytes accessed | tf_op | source)
XLA Modules:
  0.0 46.1 jit_solution(11977425208544412543)
XLA Ops:
  1.3 40.6 %shard_map.95 = (bf16[128,2048]{1,0:T(8,128)(2,1)}, f32[2,16,128]{2,1,0:T(8,128)}) custom-call(bf16[64,8,256]{2,1,0:T(8,128)(2,1)} %probes_hbm.1, f32[8,256]{1,0:T(8,128)} %vel_hbm.1, f32[8,256]{1,0:T(8,128)} %visc_hbm.1, f32[8,256]{1,0:T(8,128)} %fric_hbm.1, s32[1,64]{1,0:T(1,128)} %block_hbm.1, f32[1,64,128]{2,1,0:T(8,128)} %weight_hbm.1, f32[1,64]{1,0:T(1,128)} %prec_hbm.1), custom_call_target="tpu_custom_call" | custom-call | tf_op jit(solution)/shard_map/pallas_call | solution.py:656
  41.9 4.2 %shard_map.96 = (f32[512,256]{1,0:T(8,128)}, f32[64,64]{1,0:T(8,128)}) custom-call(f32[2,16,128]{2,1,0:T(8,128)} %get-tuple-element.6.gram_hbm, bf16[128,2048]{1,0:T(8,128)(2,1)} %get-tuple-element.7.xcat_hbm, s32[1]{0:T(128)S(6)} %copy.10.rank_hbm), custom_call_target="tpu_custom_call" | custom-call | tf_op jit(solution)/shard_map/pallas_call | solution.py:701

commit v5 on v4

--- a/solution.py
+++ b/solution.py
@@ -10,7 +10,7 @@
 BLOCK = 128
 PRIOR = 1.0
 Z_RING = 16
-NEAR = 2
+NEAR = 1
 PIVOTS = 8
 WEIGHT_STEPS = 65534.0
 PREC_STEPS = 32768.0
@@ -64,7 +64,9 @@
     forced,
     coef,
     tiles,
-    tiles_halo,
+    edge_rows,
+    rows_halo,
+    cols_halo,
     prow,
     prow_halo,
     fcol,
@@ -97,7 +99,7 @@
     piece = part.shape[1]
     nx = n_obs // 2
     groups = probe_count // 8
-    WALL, CHIP, PLANE, ZS, BOTH, TILES, FORCED, SOURCE = 0, 1, 2, 3, 4, 5, 9, 13
+    WALL, RELAY, CHIP, PLANE, ZS, BOTH, TILES, FORCED, SOURCE = 0, 1, 2, 3, 4, 5, 6, 10, 14
 
     m = lax.axis_index("mesh")
     o = lax.axis_index("obs")
@@ -112,10 +114,12 @@
         {"obs": lax.rem(o + n_obs - 1, n_obs)},
         {"obs": lax.rem(o + 1, n_obs)},
     )
-    obs_peers = [
-        {"obs": lax.rem(o + d, n_obs)}
-        for d in sorted(range(1, n_obs), key=lambda d: -min(d, n_obs - d))
-    ]
+
+    def chip_of(d):
+        same = lax.rem(o + 2 * (d % nx), n_obs)
+        return {"obs": same}, {"obs": same + 1 - 2 * core}
+
+    chips = [chip_of(d) for d in ((1, nx - 1) if nx > 2 else (1,))]
     plane_peers = [
         {"mesh": lax.rem(y + dy, ny) * nz + z, "obs": lax.rem(o + 2 * dx, n_obs)}
         for dx, dy in sorted(
@@ -123,7 +127,9 @@
             key=lambda d: -min(d[0], nx - d[0]) - min(d[1], ny - d[1]),
         )
     ]
-    y_peers = [{"mesh": lax.rem(y + d, ny) * nz + z} for d in range(1, ny)]
+
+    def y_peer(d):
+        return {"mesh": lax.rem(y + d, ny) * nz + z}
 
     def z_peer(d):
         return {"mesh": y * nz + lax.rem(z + d, nz)}
@@ -137,13 +143,11 @@
         pltpu.make_async_copy(src, dst, load_sem.at[i])
         for i, (src, dst) in enumerate(zip(names, places))
     ]
-    for load in loads:
-        load.start()
-
     barrier = pltpu.get_barrier_semaphore()
     inner = (m > 0, m < n_mesh - 1, o > 0, o < n_obs - 1)
     over_wrap = (inner[NORTH] & (z == 0), inner[SOUTH] & (z == nz - 1))
-    partners = obs_peers + y_peers + near_z
+    partners = [peer for pair in chips for peer in pair] + near_z
+    partners += [y_peer(d) for d in sorted({1, ny - 1})] + [sibling]
     for peer in partners:
         pl.semaphore_signal(barrier, inc=1, device_id=peer, device_id_type=MESH)
     for side in (NORTH, SOUTH):
@@ -154,12 +158,15 @@
                 barrier, inc=1, device_id=neighbours[side], device_id_type=MESH
             )
 
-    rows_in, columns_in = (prow_halo, srow_halo), (fcol_halo, scol_halo)
+    for load in loads:
+        load.start()
+
+    rows_in = (rows_halo, prow_halo, srow_halo)
+    columns_in = (cols_halo, fcol_halo, scol_halo)
     for side in range(4):
 
         @pl.when(jnp.logical_not(inner[side]))
         def _():
-            tiles_halo[side] = jnp.zeros((2, rows, cols), F32)
             for buf in columns_in if side >= WEST else rows_in:
                 buf[side % 2] = jnp.zeros(buf.shape[1:], buf.dtype)
 
@@ -211,6 +218,9 @@
                 prow[0, :, at] = parts[h].astype(BF16)
             if r == rows - 1:
                 prow[1, :, at] = parts[h].astype(BF16)
+    eight = lax.broadcasted_iota(jnp.int32, (8, cols), 0)
+    for i, r in enumerate((0, rows - 1)):
+        edge_rows[i] = jnp.where(eight == 0, tiles[0, r : r + 1, :], tiles[1, r : r + 1, :])
     fcol[0] = packed_edges(forced, True)
     fcol[1] = packed_edges(forced, False)
 
@@ -269,14 +279,24 @@
         def _():
             whole(buf, stage + side).wait_recv()
 
-    for side in range(4):
-        to_neighbour(tiles, tiles_halo.at[OPPOSITE[side]], TILES, side)
+    relays = nx == 4
+    if relays:
+        ahead, behind = lax.rem(o + 2 - 4 * core + n_obs, n_obs), lax.rem(o - 2 + 4 * core + n_obs, n_obs)
+        for pair, relay_core in zip(chips, (0, 1)):
+            stage = jnp.where(core == relay_core, RELAY, WALL)
+            send(wall.at[o], wall.at[o], stage, pair[0])
+    for pair in chips:
+        for peer in pair[1:] if relays else pair:
+            send(wall.at[o], wall.at[o], WALL, peer)
+    send(wall.at[o], wall.at[o], WALL, sibling)
+    for i in range(2):
+        edge = pl.ds(0, BLOCK) if i == 0 else pl.ds(cols - BLOCK, BLOCK)
+        to_neighbour(tiles.at[0, :, edge], cols_halo.at[1 - i], TILES, WEST + i)
+        to_neighbour(edge_rows.at[i], rows_halo.at[1 - i], TILES, NORTH + i)
     for i in range(2):
         to_neighbour(fcol.at[i], fcol_halo.at[1 - i], FORCED, WEST + i)
     for i in range(2):
         to_neighbour(prow.at[i], prow_halo.at[1 - i], FORCED, NORTH + i)
-    for peer in obs_peers:
-        send(wall.at[o], wall.at[o], WALL, peer)
 
     tokens = []
     reach = NEAR
@@ -294,27 +314,47 @@
         for side in range(2):
             pl.semaphore_wait(z_token.at[level, side], 1)
 
-    for d in range(1, ny):
-        pl.semaphore_signal(
-            y_token.at[d - 1], inc=1, device_id=y_peers[d - 1], device_id_type=MESH
-        )
+    def advance(level):
+        if level < len(tokens):
+            hear(level)
+            if level + 1 < len(tokens):
+                tell(level + 1)
+
+    def tell_y(level):
+        for side, d in enumerate((1, ny - 1)):
+            pl.semaphore_signal(
+                y_token.at[level, side], inc=1, device_id=y_peer(d), device_id_type=MESH
+            )
+
+    def hear_y(level):
+        for side in range(2):
+            pl.semaphore_wait(y_token.at[level, side], 1)
+
     if tokens:
         tell(0)
-
-    for side in range(4):
-        from_neighbour(tiles_halo.at[side], TILES, side)
+    if relays:
+        arrived(wall.at[behind], RELAY)
+        for peer in ({"obs": ahead}, {"obs": ahead + 1 - 2 * core}):
+            send(wall.at[behind], wall.at[behind], WALL, peer)
+
+    for i in range(2):
+        from_neighbour(rows_halo.at[i], TILES, NORTH + i)
+        from_neighbour(cols_halo.at[i], TILES, WEST + i)
     row_id = lax.broadcasted_iota(jnp.int32, (rows, cols), 0)
     col_id = lax.broadcasted_iota(jnp.int32, (rows, cols), 1)
     visc = tiles[0]
 
-    def face(side, shift, axis, edge):
-        ghost = jnp.where(inner[side], pltpu.roll(tiles_halo[side, 0], shift, axis), 0.0)
+    def face(side, ghost, shift, axis, edge):
+        ghost = jnp.where(inner[side], ghost, 0.0)
         return 0.5 * (visc + jnp.where(edge, ghost, pltpu.roll(visc, shift, axis)))
 
-    face_n = face(NORTH, 1, 0, row_id == 0)
-    face_s = face(SOUTH, rows - 1, 0, row_id == rows - 1)
-    face_w = face(WEST, 1, 1, col_id == 0)
-    face_e = face(EAST, cols - 1, 1, col_id == cols - 1)
+    from_west, from_east = shifted(cols_halo[0], 1), shifted(cols_halo[1], -1)
+    face_n = face(NORTH, rows_halo[0, 0:1, :], 1, 0, row_id == 0)
+    face_s = face(SOUTH, rows_halo[1, 0:1, :], rows - 1, 0, row_id == rows - 1)
+    face_w = face(WEST, jnp.concatenate([from_west] * halves, axis=1), 1, 1, col_id == 0)
+    face_e = face(
+        EAST, jnp.concatenate([from_east] * halves, axis=1), cols - 1, 1, col_id == cols - 1
+    )
     coef[0] = fric_ref[...] + face_n + face_s + face_w + face_e
     coef[1] = jnp.where(inner[NORTH] | (row_id > 0), face_n, 0.0)
     coef[2] = jnp.where(inner[SOUTH] | (row_id < rows - 1), face_s, 0.0)
@@ -372,22 +412,20 @@
         for h in range(halves):
             at = slice(h * BLOCK, (h + 1) * BLOCK)
             if r == 0:
-                scale = coef[1, 0:1, at] * tiles_halo[NORTH, 1, rows - 1 : rows, at]
+                scale = coef[1, 0:1, at] * rows_halo[0, 1:2, at]
                 out[h] = out[h] - scale * prow_halo[0, :, at].astype(F32)
             if r == rows - 1:
-                scale = coef[2, r : r + 1, at] * tiles_halo[SOUTH, 1, 0:1, at]
+                scale = coef[2, r : r + 1, at] * rows_halo[1, 1:2, at]
                 out[h] = out[h] - scale * prow_halo[1, :, at].astype(F32)
             tcat[h, here, 0:BLOCK] = out[h].astype(BF16)
             tcat[h, here, BLOCK : 2 * BLOCK] = out[h].astype(BF16)
 
     for r in order[2:]:
         tangent(r)
-    if tokens:
-        hear(0)
-        for level in range(1, len(tokens)):
-            tell(level)
-
-    arrived(wall.at[pl.ds(0, n_obs - 1)], WALL)
+    advance(0)
+
+    arrived(wall.at[pl.ds(0, n_obs - 1 - relays)], WALL)
+    tell_y(0)
     for i in range(n_obs):
         w_high, w_low = split(wall[i, 0:per_dev, :].astype(jnp.int32).astype(F32))
         wcat[i * per_dev : (i + 1) * per_dev, 0:BLOCK] = w_high
@@ -434,6 +472,10 @@
     scol[1] = packed_edges(field, False)
     for i in range(2):
         to_neighbour(scol.at[i], scol_halo.at[1 - i], SOURCE, WEST + i)
+
+    advance(1)
+    hear_y(0)
+    tell_y(1)
 
     for r in range(rows):
         left, right = interior(field, r)
@@ -486,16 +528,13 @@
         return values[0]
 
     send(part.at[1 - core], chip_buf, CHIP, sibling)
-    for d in range(1, ny):
-        pl.semaphore_wait(y_token.at[d - 1], 1)
+    hear_y(1)
     arrived(chip_buf, CHIP)
     here = y * nx + x
     plane_buf[here] = part[core] + chip_buf[...]
     for peer in plane_peers:
         send(plane_buf.at[here], plane_buf.at[here], PLANE, peer)
-    if tokens:
-        for level in range(1, len(tokens)):
-            hear(level)
+    advance(2)
     arrived(plane_buf.at[pl.ds(0, nx * ny - 1)], PLANE)
     z_buf[z] = total(plane_buf, nx * ny)
     for peer in z_peers:
@@ -672,7 +711,9 @@
             pltpu.VMEM((rows, probe_count, cols), F32),
             pltpu.VMEM((7, rows, cols), F32),
             pltpu.VMEM((2, rows, cols), F32),
-            pltpu.VMEM((4, 2, rows, cols), F32),
+            pltpu.VMEM((2, 8, cols), F32),
+            pltpu.VMEM((2, 8, cols), F32),
+            pltpu.VMEM((2, rows, BLOCK), F32),
             pltpu.VMEM((2, probe_count, cols), BF16),
             pltpu.VMEM((2, probe_count, cols), BF16),
             pltpu.VMEM((2, 8, BLOCK), F32),
@@ -691,10 +732,10 @@
             pltpu.VMEM((nz, piece, BLOCK), F32),
             pltpu.VMEM((2, piece, BLOCK), F32),
             dma((7,)),
-            dma((17,)),
-            dma((17,)),
+            dma((18,)),
+            dma((18,)),
+            pltpu.SemaphoreType.REGULAR((3, 2)),
             pltpu.SemaphoreType.REGULAR((2, 2)),
-            pltpu.SemaphoreType.REGULAR((max(ny - 1, 1),)),
         ],
         compiler_params=pltpu.CompilerParams(collective_id=0, has_side_effects=True),
     )(probes, velocity, viscosity, friction, obs_block, obs_weight, obs_prec)

time: 46.3 us -> 48.2 us (1.041)
  Pallas kernels: 44.8 us -> 46.7 us
    pallas_call x1, Pallas kernels: 40.6 us -> 42.4 us  [per_device(): pl.pallas_call(functools.partial(sketch_kernel, n_mesh, n_obs, nz), out_s...]
where the time goes in v5:
time: 48.2 us; the launch traced here: 47.9 us
  Pallas kernels  46.7 us (97%)
  between operations  1.29 us (3%)
    pallas_call x1, Pallas kernels, per_device(): pl.pallas_call(functools.partial(sketch_kernel, n_mesh, n_obs, nz), out_s...  42.4 us
    pallas_call x1, Pallas kernels, per_device(): pl.pallas_call(basis_kernel, out_shape=(jax.ShapeDtypeStruct((probe_count...  4.25 us

profile of v5, /device:TPU:1, one launch (start us, length us, event | category | flops | bytes accessed | tf_op | source)
XLA Modules:
  0.0 47.9 jit_solution(15625295715612650002)
XLA Ops:
  1.3 42.4 %shard_map.95 = (bf16[128,2048]{1,0:T(8,128)(2,1)}, f32[2,16,128]{2,1,0:T(8,128)}) custom-call(bf16[64,8,256]{2,1,0:T(8,128)(2,1)} %probes_hbm.1, f32[8,256]{1,0:T(8,128)} %vel_hbm.1, f32[8,256]{1,0:T(8,128)} %visc_hbm.1, f32[8,256]{1,0:T(8,128)} %fric_hbm.1, s32[1,64]{1,0:T(1,128)} %block_hbm.1, f32[1,64,128]{2,1,0:T(8,128)} %weight_hbm.1, f32[1,64]{1,0:T(1,128)} %prec_hbm.1), custom_call_target="tpu_custom_call" | custom-call | tf_op jit(solution)/shard_map/pallas_call | solution.py:695
  43.7 4.2 %shard_map.96 = (f32[512,256]{1,0:T(8,128)}, f32[64,64]{1,0:T(8,128)}) custom-call(f32[2,16,128]{2,1,0:T(8,128)} %get-tuple-element.6.gram_hbm, bf16[128,2048]{1,0:T(8,128)(2,1)} %get-tuple-element.7.xcat_hbm, s32[1]{0:T(128)S(6)} %copy.10.rank_hbm), custom_call_target="tpu_custom_call" | custom-call | tf_op jit(solution)/shard_map/pallas_call | solution.py:742

commit v6 on v5

--- a/solution.py
+++ b/solution.py
@@ -71,6 +71,7 @@
     prow_halo,
     fcol,
     fcol_halo,
+    srow,
     srow_halo,
     scol,
     scol_halo,
@@ -99,7 +100,7 @@
     piece = part.shape[1]
     nx = n_obs // 2
     groups = probe_count // 8
-    WALL, RELAY, CHIP, PLANE, ZS, BOTH, TILES, FORCED, SOURCE = 0, 1, 2, 3, 4, 5, 6, 10, 14
+    WALL, CHIP, PLANE, ZS, BOTH, TILES, FORCED, SOURCE = 0, 1, 2, 3, 4, 5, 9, 13
 
     m = lax.axis_index("mesh")
     o = lax.axis_index("obs")
@@ -114,12 +115,10 @@
         {"obs": lax.rem(o + n_obs - 1, n_obs)},
         {"obs": lax.rem(o + 1, n_obs)},
     )
-
-    def chip_of(d):
-        same = lax.rem(o + 2 * (d % nx), n_obs)
-        return {"obs": same}, {"obs": same + 1 - 2 * core}
-
-    chips = [chip_of(d) for d in ((1, nx - 1) if nx > 2 else (1,))]
+    obs_peers = [
+        {"obs": lax.rem(o + d, n_obs)}
+        for d in sorted(range(1, n_obs), key=lambda d: -min(d, n_obs - d))
+    ]
     plane_peers = [
         {"mesh": lax.rem(y + dy, ny) * nz + z, "obs": lax.rem(o + 2 * dx, n_obs)}
         for dx, dy in sorted(
@@ -146,8 +145,7 @@
     barrier = pltpu.get_barrier_semaphore()
     inner = (m > 0, m < n_mesh - 1, o > 0, o < n_obs - 1)
     over_wrap = (inner[NORTH] & (z == 0), inner[SOUTH] & (z == nz - 1))
-    partners = [peer for pair in chips for peer in pair] + near_z
-    partners += [y_peer(d) for d in sorted({1, ny - 1})] + [sibling]
+    partners = obs_peers + [y_peer(d) for d in sorted({1, ny - 1})] + near_z
     for peer in partners:
         pl.semaphore_signal(barrier, inc=1, device_id=peer, device_id_type=MESH)
     for side in (NORTH, SOUTH):
@@ -279,24 +277,15 @@
         def _():
             whole(buf, stage + side).wait_recv()
 
-    relays = nx == 4
-    if relays:
-        ahead, behind = lax.rem(o + 2 - 4 * core + n_obs, n_obs), lax.rem(o - 2 + 4 * core + n_obs, n_obs)
-        for pair, relay_core in zip(chips, (0, 1)):
-            stage = jnp.where(core == relay_core, RELAY, WALL)
-            send(wall.at[o], wall.at[o], stage, pair[0])
-    for pair in chips:
-        for peer in pair[1:] if relays else pair:
-            send(wall.at[o], wall.at[o], WALL, peer)
-    send(wall.at[o], wall.at[o], WALL, sibling)
     for i in range(2):
         edge = pl.ds(0, BLOCK) if i == 0 else pl.ds(cols - BLOCK, BLOCK)
         to_neighbour(tiles.at[0, :, edge], cols_halo.at[1 - i], TILES, WEST + i)
         to_neighbour(edge_rows.at[i], rows_halo.at[1 - i], TILES, NORTH + i)
     for i in range(2):
+        to_neighbour(prow.at[i], prow_halo.at[1 - i], FORCED, NORTH + i)
         to_neighbour(fcol.at[i], fcol_halo.at[1 - i], FORCED, WEST + i)
-    for i in range(2):
-        to_neighbour(prow.at[i], prow_halo.at[1 - i], FORCED, NORTH + i)
+    for peer in obs_peers:
+        send(wall.at[o], wall.at[o], WALL, peer)
 
     tokens = []
     reach = NEAR
@@ -332,10 +321,7 @@
 
     if tokens:
         tell(0)
-    if relays:
-        arrived(wall.at[behind], RELAY)
-        for peer in ({"obs": ahead}, {"obs": ahead + 1 - 2 * core}):
-            send(wall.at[behind], wall.at[behind], WALL, peer)
+    tell_y(0)
 
     for i in range(2):
         from_neighbour(rows_halo.at[i], TILES, NORTH + i)
@@ -424,8 +410,7 @@
         tangent(r)
     advance(0)
 
-    arrived(wall.at[pl.ds(0, n_obs - 1 - relays)], WALL)
-    tell_y(0)
+    arrived(wall.at[pl.ds(0, n_obs - 1)], WALL)
     for i in range(n_obs):
         w_high, w_low = split(wall[i, 0:per_dev, :].astype(jnp.int32).astype(F32))
         wcat[i * per_dev : (i + 1) * per_dev, 0:BLOCK] = w_high
@@ -467,7 +452,8 @@
                 ]
         if group[0] == 0:
             for i in range(2):
-                to_neighbour(field.at[(rows - 1) * i], srow_halo.at[1 - i], SOURCE, NORTH + i)
+                srow[i] = field[(rows - 1) * i].astype(BF16)
+                to_neighbour(srow.at[i], srow_halo.at[1 - i], SOURCE, NORTH + i)
     scol[0] = packed_edges(field, True)
     scol[1] = packed_edges(field, False)
     for i in range(2):
@@ -495,9 +481,9 @@
             for h in range(halves):
                 at = slice(h * BLOCK, (h + 1) * BLOCK)
                 if r == 0:
-                    out[h] = out[h] - coef[1, 0:1, at] * srow_halo[0, :, at]
+                    out[h] = out[h] - coef[1, 0:1, at] * srow_halo[0, :, at].astype(F32)
                 if r == rows - 1:
-                    out[h] = out[h] - coef[2, r : r + 1, at] * srow_halo[1, :, at]
+                    out[h] = out[h] - coef[2, r : r + 1, at] * srow_halo[1, :, at].astype(F32)
                 s_high, s_low = split(tiles[1, r : r + 1, at] * out[h] + PRIOR * parts[h])
                 here = slice(r * cols + h * BLOCK, r * cols + (h + 1) * BLOCK)
                 xcat[0:probe_count, here] = s_high
@@ -718,7 +704,8 @@
             pltpu.VMEM((2, probe_count, cols), BF16),
             pltpu.VMEM((2, 8, BLOCK), F32),
             pltpu.VMEM((2, 8, BLOCK), F32),
-            pltpu.VMEM((2, probe_count, cols), F32),
+            pltpu.VMEM((2, probe_count, cols), BF16),
+            pltpu.VMEM((2, probe_count, cols), BF16),
             pltpu.VMEM((2, 8, BLOCK), F32),
             pltpu.VMEM((2, 8, BLOCK), F32),
             pltpu.VMEM((16, BLOCK), F32),
@@ -732,8 +719,8 @@
             pltpu.VMEM((nz, piece, BLOCK), F32),
             pltpu.VMEM((2, piece, BLOCK), F32),
             dma((7,)),
-            dma((18,)),
-            dma((18,)),
+            dma((17,)),
+            dma((17,)),
             pltpu.SemaphoreType.REGULAR((3, 2)),
             pltpu.SemaphoreType.REGULAR((2, 2)),
         ],

time: 48.2 us -> 45.5 us (0.944)
  Pallas kernels: 46.7 us -> 44 us
    pallas_call x1, Pallas kernels: 42.4 us -> 39.8 us  [per_device(): pl.pallas_call(functools.partial(sketch_kernel, n_mesh, n_obs, nz), out_s...]
where the time goes in v6:
time: 45.5 us; the launch traced here: 45.3 us
  Pallas kernels  44 us (97%)
  between operations  1.29 us (3%)
    pallas_call x1, Pallas kernels, per_device(): pl.pallas_call(functools.partial(sketch_kernel, n_mesh, n_obs, nz), out_s...  39.8 us
    pallas_call x1, Pallas kernels, per_device(): pl.pallas_call(basis_kernel, out_shape=(jax.ShapeDtypeStruct((probe_count...  4.25 us

profile of v6, /device:TPU:1, one launch (start us, length us, event | category | flops | bytes accessed | tf_op | source)
XLA Modules:
  0.0 45.3 jit_solution(4827815640902979083)
XLA Ops:
  1.3 39.8 %shard_map.95 = (bf16[128,2048]{1,0:T(8,128)(2,1)}, f32[2,16,128]{2,1,0:T(8,128)}) custom-call(bf16[64,8,256]{2,1,0:T(8,128)(2,1)} %probes_hbm.1, f32[8,256]{1,0:T(8,128)} %vel_hbm.1, f32[8,256]{1,0:T(8,128)} %visc_hbm.1, f32[8,256]{1,0:T(8,128)} %fric_hbm.1, s32[1,64]{1,0:T(1,128)} %block_hbm.1, f32[1,64,128]{2,1,0:T(8,128)} %weight_hbm.1, f32[1,64]{1,0:T(1,128)} %prec_hbm.1), custom_call_target="tpu_custom_call" | custom-call | tf_op jit(solution)/shard_map/pallas_call | solution.py:681
  41.1 4.2 %shard_map.96 = (f32[512,256]{1,0:T(8,128)}, f32[64,64]{1,0:T(8,128)}) custom-call(f32[2,16,128]{2,1,0:T(8,128)} %get-tuple-element.6.gram_hbm, bf16[128,2048]{1,0:T(8,128)(2,1)} %get-tuple-element.7.xcat_hbm, s32[1]{0:T(128)S(6)} %copy.10.rank_hbm), custom_call_target="tpu_custom_call" | custom-call | tf_op jit(solution)/shard_map/pallas_call | solution.py:729

commit v7 on v6

--- a/solution.py
+++ b/solution.py
@@ -282,10 +282,11 @@
         to_neighbour(tiles.at[0, :, edge], cols_halo.at[1 - i], TILES, WEST + i)
         to_neighbour(edge_rows.at[i], rows_halo.at[1 - i], TILES, NORTH + i)
     for i in range(2):
-        to_neighbour(prow.at[i], prow_halo.at[1 - i], FORCED, NORTH + i)
         to_neighbour(fcol.at[i], fcol_halo.at[1 - i], FORCED, WEST + i)
     for peer in obs_peers:
         send(wall.at[o], wall.at[o], WALL, peer)
+    for i in range(2):
+        to_neighbour(prow.at[i], prow_halo.at[1 - i], FORCED, NORTH + i)
 
     tokens = []
     reach = NEAR

time: 45.5 us -> 45.5 us (level)
  no operation moved by 1% of the time
where the time goes in v7:
time: 45.5 us; the launch traced here: 45.3 us
  Pallas kernels  44 us (97%)
  between operations  1.29 us (3%)
    pallas_call x1, Pallas kernels, per_device(): pl.pallas_call(functools.partial(sketch_kernel, n_mesh, n_obs, nz), out_s...  39.8 us
    pallas_call x1, Pallas kernels, per_device(): pl.pallas_call(basis_kernel, out_shape=(jax.ShapeDtypeStruct((probe_count...  4.25 us

profile of v7, /device:TPU:1, one launch (start us, length us, event | category | flops | bytes accessed | tf_op | source)
XLA Modules:
  0.0 45.3 jit_solution(14834893589413624106)
XLA Ops:
  1.3 39.8 %shard_map.95 = (bf16[128,2048]{1,0:T(8,128)(2,1)}, f32[2,16,128]{2,1,0:T(8,128)}) custom-call(bf16[64,8,256]{2,1,0:T(8,128)(2,1)} %probes_hbm.1, f32[8,256]{1,0:T(8,128)} %vel_hbm.1, f32[8,256]{1,0:T(8,128)} %visc_hbm.1, f32[8,256]{1,0:T(8,128)} %fric_hbm.1, s32[1,64]{1,0:T(1,128)} %block_hbm.1, f32[1,64,128]{2,1,0:T(8,128)} %weight_hbm.1, f32[1,64]{1,0:T(1,128)} %prec_hbm.1), custom_call_target="tpu_custom_call" | custom-call | tf_op jit(solution)/shard_map/pallas_call | solution.py:682
  41.1 4.2 %shard_map.96 = (f32[512,256]{1,0:T(8,128)}, f32[64,64]{1,0:T(8,128)}) custom-call(f32[2,16,128]{2,1,0:T(8,128)} %get-tuple-element.6.gram_hbm, bf16[128,2048]{1,0:T(8,128)(2,1)} %get-tuple-element.7.xcat_hbm, s32[1]{0:T(128)S(6)} %copy.10.rank_hbm), custom_call_target="tpu_custom_call" | custom-call | tf_op jit(solution)/shard_map/pallas_call | solution.py:730

commit v8 on v7

--- a/solution.py
+++ b/solution.py
@@ -460,14 +460,13 @@
     for i in range(2):
         to_neighbour(scol.at[i], scol_halo.at[1 - i], SOURCE, WEST + i)
 
-    advance(1)
-    hear_y(0)
-    tell_y(1)
-
     for r in range(rows):
         left, right = interior(field, r)
         forced[r, :, 0:BLOCK] = left
         forced[r, :, BLOCK:cols] = right
+    advance(1)
+    hear_y(0)
+    tell_y(1)
     for i in range(2):
         from_neighbour(scol_halo.at[i], SOURCE, WEST + i)
     columns = spread(scol_halo)
@@ -526,6 +525,16 @@
     z_buf[z] = total(plane_buf, nx * ny)
     for peer in z_peers:
         send(z_buf.at[z], z_buf.at[z], ZS, peer)
+    for copy in unsent:
+        copy.wait_send()
+    for src, at, side in edge_copies:
+
+        @pl.when(inner[side])
+        def _():
+            whole(src, at).wait_send()
+
+    keep_sketch.wait()
+    done = len(unsent)
     arrived(z_buf.at[pl.ds(0, nz - 1)], ZS)
     cells = rows * cols * n_mesh * n_obs
     both_buf[core] = total(z_buf, nz) / cells
@@ -533,15 +542,8 @@
     arrived(both_buf.at[0], BOTH)
     keep_gram = pltpu.make_async_copy(both_buf, gram_hbm, load_sem.at[1])
     keep_gram.start()
-    for copy in unsent:
+    for copy in unsent[done:]:
         copy.wait_send()
-    for src, at, side in edge_copies:
-
-        @pl.when(inner[side])
-        def _():
-            whole(src, at).wait_send()
-
-    keep_sketch.wait()
     keep_gram.wait()
 
 

time: 45.5 us -> 45.3 us (level)
  no operation moved by 1% of the time
where the time goes in v8:
time: 45.3 us; the launch traced here: 45 us
  Pallas kernels  43.7 us (96%)
  between operations  1.29 us (3%)
    pallas_call x1, Pallas kernels, per_device(): pl.pallas_call(functools.partial(sketch_kernel, n_mesh, n_obs, nz), out_s...  39.5 us
    pallas_call x1, Pallas kernels, per_device(): pl.pallas_call(basis_kernel, out_shape=(jax.ShapeDtypeStruct((probe_count...  4.25 us

profile of v8, /device:TPU:1, one launch (start us, length us, event | category | flops | bytes accessed | tf_op | source)
XLA Modules:
  0.0 45.0 jit_solution(10517426649355777722)
XLA Ops:
  1.3 39.5 %shard_map.95 = (bf16[128,2048]{1,0:T(8,128)(2,1)}, f32[2,16,128]{2,1,0:T(8,128)}) custom-call(bf16[64,8,256]{2,1,0:T(8,128)(2,1)} %probes_hbm.1, f32[8,256]{1,0:T(8,128)} %vel_hbm.1, f32[8,256]{1,0:T(8,128)} %visc_hbm.1, f32[8,256]{1,0:T(8,128)} %fric_hbm.1, s32[1,64]{1,0:T(1,128)} %block_hbm.1, f32[1,64,128]{2,1,0:T(8,128)} %weight_hbm.1, f32[1,64]{1,0:T(1,128)} %prec_hbm.1), custom_call_target="tpu_custom_call" | custom-call | tf_op jit(solution)/shard_map/pallas_call | solution.py:684
  40.8 4.2 %shard_map.96 = (f32[512,256]{1,0:T(8,128)}, f32[64,64]{1,0:T(8,128)}) custom-call(f32[2,16,128]{2,1,0:T(8,128)} %get-tuple-element.6.gram_hbm, bf16[128,2048]{1,0:T(8,128)(2,1)} %get-tuple-element.7.xcat_hbm, s32[1]{0:T(128)S(6)} %copy.10.rank_hbm), custom_call_target="tpu_custom_call" | custom-call | tf_op jit(solution)/shard_map/pallas_call | solution.py:732

commit v9 on v8

--- a/solution.py
+++ b/solution.py
@@ -142,6 +142,9 @@
         pltpu.make_async_copy(src, dst, load_sem.at[i])
         for i, (src, dst) in enumerate(zip(names, places))
     ]
+    for load in loads:
+        load.start()
+
     barrier = pltpu.get_barrier_semaphore()
     inner = (m > 0, m < n_mesh - 1, o > 0, o < n_obs - 1)
     over_wrap = (inner[NORTH] & (z == 0), inner[SOUTH] & (z == nz - 1))
@@ -155,9 +158,6 @@
             pl.semaphore_signal(
                 barrier, inc=1, device_id=neighbours[side], device_id_type=MESH
             )
-
-    for load in loads:
-        load.start()
 
     rows_in = (rows_halo, prow_halo, srow_halo)
     columns_in = (cols_halo, fcol_halo, scol_halo)

time: 45.3 us -> 45.3 us (level)
  no operation moved by 1% of the time
where the time goes in v9:
time: 45.3 us; the launch traced here: 45 us
  Pallas kernels  43.8 us (97%)
  between operations  1.29 us (3%)
    pallas_call x1, Pallas kernels, per_device(): pl.pallas_call(functools.partial(sketch_kernel, n_mesh, n_obs, nz), out_s...  39.5 us
    pallas_call x1, Pallas kernels, per_device(): pl.pallas_call(basis_kernel, out_shape=(jax.ShapeDtypeStruct((probe_count...  4.25 us

profile of v9, /device:TPU:1, one launch (start us, length us, event | category | flops | bytes accessed | tf_op | source)
XLA Modules:
  0.0 45.0 jit_solution(8096426919924688455)
XLA Ops:
  1.3 39.5 %shard_map.95 = (bf16[128,2048]{1,0:T(8,128)(2,1)}, f32[2,16,128]{2,1,0:T(8,128)}) custom-call(bf16[64,8,256]{2,1,0:T(8,128)(2,1)} %probes_hbm.1, f32[8,256]{1,0:T(8,128)} %vel_hbm.1, f32[8,256]{1,0:T(8,128)} %visc_hbm.1, f32[8,256]{1,0:T(8,128)} %fric_hbm.1, s32[1,64]{1,0:T(1,128)} %block_hbm.1, f32[1,64,128]{2,1,0:T(8,128)} %weight_hbm.1, f32[1,64]{1,0:T(1,128)} %prec_hbm.1), custom_call_target="tpu_custom_call" | custom-call | tf_op jit(solution)/shard_map/pallas_call | solution.py:684
  40.8 4.2 %shard_map.96 = (f32[512,256]{1,0:T(8,128)}, f32[64,64]{1,0:T(8,128)}) custom-call(f32[2,16,128]{2,1,0:T(8,128)} %get-tuple-element.6.gram_hbm, bf16[128,2048]{1,0:T(8,128)(2,1)} %get-tuple-element.7.xcat_hbm, s32[1]{0:T(128)S(6)} %copy.10.rank_hbm), custom_call_target="tpu_custom_call" | custom-call | tf_op jit(solution)/shard_map/pallas_call | solution.py:732
